TPU v7x, 256 devices: a whole 4x4x8 slice. The times are simulated.
256 devices in a mesh: seq: 32 (over y, x, core), head: 8 (over z).
Axes of the slice: x: 4, y: 4, z: 8, core: 2. Of those that a mesh axis runs over, the one named last changes fastest.
Arguments:
- query_rows: bfloat16 [16384, 4096], P('seq', 'head'), may hold values from -6 to 6
- key_rows: bfloat16 [16384, 4096], P('seq', 'head'), may hold values from -6 to 6
- value_rows: bfloat16 [16384, 4096], P('seq', 'head'), may hold values from -6 to 6
- out_weight: bfloat16 [4096, 4096], P('seq', 'head'), may hold values from -0.09375 to 0.09375
- target_rows: bfloat16 [16384, 4096], P('seq', 'head'), may hold values from -6 to 6
Outputs:
- output: bfloat16 [16384, 4096], P('seq', 'head')
- grad_query: bfloat16 [16384, 4096], P('seq', 'head')
- grad_key: bfloat16 [16384, 4096], P('seq', 'head')
- grad_value: bfloat16 [16384, 4096], P('seq', 'head')
- grad_weight: float32 [4096, 4096], P('seq', 'head')
All inputs are finite; a program needn't handle non-finite values.
Results may differ from a plain program's by a relative error of at most 0.019.
Values may be sent and summed in bfloat16 or wider, within the bound.
A program may use at most 64 MiB of HBM per device.

v0:
```python
import math

import jax
import jax.numpy as jnp
from jax import lax
from jax.sharding import Mesh
from jax.sharding import PartitionSpec as P

DH = 128
BLK = 512
SEQ = ("seq_0", "seq_1", "seq_2")


EXACT = lax.Precision.HIGHEST


def filled_with(x, identity):
    return jnp.broadcast_to(jnp.asarray(identity, x.dtype), x.shape)


def entering(x, axes, combine, identity, reverse):
    before = start = filled_with(x, identity)
    so_far = x
    for axis in reversed(axes):
        devices, place = (lax.axis_size(axis), lax.axis_index(axis))
        pieces = lax.all_gather(so_far.astype(jnp.bfloat16), axis)
        inside, so_far = (start, start)
        for k in reversed(range(devices)) if reverse else range(devices):
            passed = k > place if reverse else k < place
            so_far = combine(so_far, pieces[k].astype(x.dtype))
            inside = jnp.where(passed, so_far, inside)
        before = combine(inside, before)
    return before


def add_states(earlier, later_one):
    return earlier + later_one


def on_device(query_rows, key_rows, value_rows, out_weight, target_rows):
    rows_dev = query_rows.shape[0]
    feature_width = query_rows.shape[1]
    local_heads = feature_width // DH
    block_count = rows_dev // BLK
    seq_count = lax.axis_size(SEQ)
    total_rows = rows_dev * seq_count
    seq_index = lax.axis_index(SEQ)
    positions = (seq_index * rows_dev + jnp.arange(rows_dev, dtype=jnp.int32) + 1).astype(
        jnp.float32
    )
    query_scale = lax.rsqrt(jnp.float32(DH) * positions)
    scaled = (query_rows.astype(jnp.float32) * query_scale[:, None]).astype(jnp.bfloat16)
    shaped = (block_count, BLK, local_heads, DH)
    query_blocks = scaled.reshape(shaped)
    key_blocks = key_rows.reshape(shaped)
    value_blocks = value_rows.reshape(shaped)
    causal = jnp.tril(jnp.ones((BLK, BLK), dtype=bool))
    empty_state = jnp.zeros((local_heads, DH, DH), jnp.float32)
    block_kv = jnp.einsum(
        "bshd,bshe->bhde", key_blocks, value_blocks, preferred_element_type=jnp.float32
    )
    local_total = jnp.sum(block_kv, axis=0)
    earlier = entering(local_total, SEQ, add_states, empty_state, False)
    running_kv = jnp.cumsum(block_kv, axis=0)
    before = earlier[None] + jnp.concatenate([jnp.zeros_like(block_kv), running_kv[:-1]], axis=0)
    inter = jnp.einsum("bthd,bhde->bthe", query_blocks.astype(jnp.float32), before, precision=EXACT)
    scores = jnp.einsum(
        "bthd,bshd->bhts", query_blocks, key_blocks, preferred_element_type=jnp.float32
    )
    scores = jnp.where(causal, scores, 0.0).astype(jnp.bfloat16)
    intra = jnp.einsum("bhts,bshe->bthe", scores, value_blocks, preferred_element_type=jnp.float32)
    attended = (inter + intra).astype(jnp.bfloat16).reshape(rows_dev, feature_width)
    whole_weight = lax.all_gather(out_weight, SEQ, axis=0, tiled=True)
    partial_out = lax.dot_general(
        attended, whole_weight, (((1,), (1,)), ((), ())), preferred_element_type=jnp.float32
    )
    summed = lax.psum_scatter(
        partial_out.astype(jnp.bfloat16), "head", scatter_dimension=1, tiled=True
    )
    residual = (summed.astype(jnp.float32) - target_rows.astype(jnp.float32)).astype(jnp.bfloat16)
    residual_full = lax.all_gather(residual, "head", axis=1, tiled=True)
    grad_attended = jnp.dot(residual_full, whole_weight, preferred_element_type=jnp.float32).astype(
        jnp.bfloat16
    )
    weight_factor = 1.0 / math.sqrt(total_rows)
    product = lax.dot_general(
        residual_full, attended, (((0,), (0,)), ((), ())), preferred_element_type=jnp.float32
    )
    grad_weight = lax.psum_scatter(
        (product * weight_factor).astype(jnp.bfloat16), SEQ, scatter_dimension=0, tiled=True
    ).astype(jnp.float32)
    grad_blocks = grad_attended.reshape(shaped)
    block_qg = jnp.einsum(
        "bthd,bthe->bhde", query_blocks, grad_blocks, preferred_element_type=jnp.float32
    )
    local_grad = jnp.sum(block_qg, axis=0)
    later = entering(local_grad, SEQ, add_states, empty_state, True)
    running_qg = jnp.cumsum(block_qg[::-1], axis=0)[::-1]
    after = later[None] + jnp.concatenate([running_qg[1:], jnp.zeros_like(block_qg)], axis=0)
    mixed = jnp.einsum(
        "bthe,bshe->bhts", grad_blocks, value_blocks, preferred_element_type=jnp.float32
    )
    mixed = jnp.where(causal, mixed, 0.0).astype(jnp.bfloat16)
    grad_scaled = jnp.einsum(
        "bthe,bhde->bthd", grad_blocks.astype(jnp.float32), before, precision=EXACT
    )
    grad_scaled = grad_scaled + jnp.einsum(
        "bhts,bshd->bthd", mixed, key_blocks, preferred_element_type=jnp.float32
    )
    grad_key = jnp.einsum(
        "bshe,bhde->bshd", value_blocks.astype(jnp.float32), after, precision=EXACT
    )
    grad_key = grad_key + jnp.einsum(
        "bhts,bthd->bshd", mixed, query_blocks, preferred_element_type=jnp.float32
    )
    grad_value = jnp.einsum(
        "bshd,bhde->bshe", key_blocks.astype(jnp.float32), after, precision=EXACT
    )
    grad_value = grad_value + jnp.einsum(
        "bhts,bthe->bshe", scores, grad_blocks, preferred_element_type=jnp.float32
    )
    grad_query = (grad_scaled.reshape(rows_dev, feature_width) * query_scale[:, None]).astype(
        jnp.bfloat16
    )
    return (
        summed,
        grad_query,
        grad_key.astype(jnp.bfloat16).reshape(rows_dev, feature_width),
        grad_value.astype(jnp.bfloat16).reshape(rows_dev, feature_width),
        grad_weight,
    )


def solution(mesh):
    torus = Mesh(
        mesh.devices.reshape(4, 4, 2, mesh.shape["head"]), ("seq_0", "seq_1", "seq_2", "head")
    )
    return jax.shard_map(
        on_device,
        mesh=torus,
        in_specs=(P(SEQ, "head"), P(SEQ, "head"), P(SEQ, "head"), P(SEQ, "head"), P(SEQ, "head")),
        out_specs=(P(SEQ, "head"), P(SEQ, "head"), P(SEQ, "head"), P(SEQ, "head"), P(SEQ, "head")),
        check_vma=False,
    )
```

profile of v0, /device:TPU:16, one launch (start us, length us, event | category | flops | bytes accessed | tf_op | source)
XLA Modules:
  0.0 285.6 jit_solution(8579663501388462409)
XLA Ops:
  7.2 0.0 copy-start
  7.2 0.0 all-gather.5.cloned.1.call-start
  7.2 0.7 all-gather.5.cloned.1.call-update
  7.9 0.0 reduce-scatter.3.cloned.1.call-start
  8.0 1.3 copy.82
  9.2 0.0 copy-start.5
  9.3 1.4 multiply_convert_fusion.2
  10.7 0.2 copy.55
  10.9 0.0 copy-done
  10.9 0.3 convolution_convert_fusion.3
  11.2 2.0 all-gather
  13.2 0.1 iota_compare_fusion
  13.3 0.0 copy-start.7
  13.3 13.1 %all_gather.31 = bf16[4,4,128,128]{3,2,1,0:T(8,128)(2,1)S(1)} all-gather(bf16[1,4,128,128]{3,2,1,0:T(8,128)(2,1)S(1)} %fusion.41), channel_id=1, replica_groups=mesh['seq_0'=4,'seq_1'=4,'seq_2'=2,'head'=8] {'seq_1'}, dimensions={0}, use_global_device_ids=true | all-gather | bytes 655360 | tf_op jit(solution)/shard_map/all_gather | solution.py:26
  26.5 0.1 fusion.40
  26.5 13.4 %all_gather.32 = bf16[4,4,128,128]{3,2,1,0:T(8,128)(2,1)S(1)} all-gather(bf16[1,4,128,128]{3,2,1,0:T(8,128)(2,1)S(1)} %fusion.40), channel_id=1, replica_groups=mesh['seq_0'=4,'seq_1'=4,'seq_2'=2,'head'=8] {'seq_0'}, dimensions={0}, use_global_device_ids=true | all-gather | bytes 655360 | tf_op jit(solution)/shard_map/all_gather | solution.py:26
  39.9 0.3 fusion.20
  40.2 0.0 copy-done.5
  40.2 0.0 copy-start.3
  40.2 2.0 select_convert_fusion.1
  42.2 0.8 convolution_bitcast_fusion.1
  43.0 0.0 copy-done.7
  43.0 0.0 copy-done.3
  43.0 1.4 fusion
  44.5 19.4 %all-gather.5.cloned.1.call-done = bf16[4096,512]{1,0:T(8,128)(2,1)} async-done(((bf16[128,512]{1,0:T(8,128)(2,1)}), bf16[4096,512]{1,0:T(8,128)(2,1)}) %all-gather.5.cloned.1.call-update) | async-done | bytes 4194320 | tf_op jit(solution)/shard_map/all_gather | solution.py:73
  63.9 6.7 %convolution_convert_fusion = bf16[512,4096]{1,0:T(8,128)(2,1)} fusion(bf16[512,512]{0,1:T(8,128)(2,1)} %bitcast.114, bf16[4096,512]{1,0:T(8,128)(2,1)} %all-gather.5.cloned.1.call-done), kind=kOutput, calls=%fused_computation.1 | convolution fusion | flops 2149580800 | bytes 8912896 | tf_op jit(solution)/shard_map/dot_general | solution.py:74
  70.6 0.0 reduce-scatter.3.cloned.1.call-update
  70.6 0.0 all-gather.7.cloned.1.call-start
  70.7 55.9 %reduce-scatter.3.cloned.1.call-done = bf16[512,512]{1,0:T(8,128)(2,1)} async-done(((bf16[512,4096]{1,0:T(8,128)(2,1)}), bf16[512,512]{1,0:T(8,128)(2,1)}) %reduce-scatter.3.cloned.1.call-update) | async-done | bytes 524304 | tf_op jit(solution)/shard_map/reduce_scatter | solution.py:77
  126.6 2.1 subtract_convert_fusion
  128.7 0.0 all-gather.7.cloned.1.call-update
  128.7 0.0 reduce-scatter.5.cloned.1.call-start
  128.8 53.6 %all-gather.7.cloned.1.call-done = bf16[512,4096]{1,0:T(8,128)(2,1)} async-done(((bf16[512,512]{1,0:T(8,128)(2,1)}), bf16[512,4096]{1,0:T(8,128)(2,1)}) %all-gather.7.cloned.1.call-update) | async-done | bytes 4194320 | tf_op jit(solution)/shard_map/all_gather | solution.py:81
  182.4 6.7 %multiply_convert_fusion = bf16[4096,512]{1,0:T(8,128)(2,1)} fusion(bf16[512,4096]{1,0:T(8,128)(2,1)} %all-gather.7.cloned.1.call-done, bf16[512,512]{0,1:T(8,128)(2,1)} %bitcast.115), kind=kOutput, calls=%fused_computation | convolution fusion | flops 2151677952 | bytes 8912896 | tf_op jit(solution)/shard_map/dot_general | solution.py:86
  189.0 0.0 reduce-scatter.5.cloned.1.call-update
  189.1 5.8 %convolution_convert_fusion.1 = bf16[512,512]{0,1:T(8,128)(2,1)S(1)} fusion(bf16[512,4096]{1,0:T(8,128)(2,1)} %all-gather.7.cloned.1.call-done, bf16[4096,512]{1,0:T(8,128)(2,1)} %all-gather.5.cloned.1.call-done), kind=kOutput, calls=%fused_computation.10 | convolution fusion | flops 2147745792 | bytes 8912896 | tf_op jit(solution)/shard_map/dot_general | solution.py:82
  194.9 0.0 copy-start.1
  195.0 0.3 convolution_convert_fusion.2
  195.3 0.0 copy-start.6
  195.3 2.1 all-gather.1
  197.4 13.1 %all_gather.36 = bf16[4,4,128,128]{3,2,1,0:T(8,128)(2,1)S(1)} all-gather(bf16[1,4,128,128]{3,2,1,0:T(8,128)(2,1)S(1)} %fusion.42), channel_id=1, replica_groups=mesh['seq_0'=4,'seq_1'=4,'seq_2'=2,'head'=8] {'seq_1'}, dimensions={0}, use_global_device_ids=true | all-gather | bytes 655360 | tf_op jit(solution)/shard_map/all_gather | solution.py:26
  210.5 0.1 fusion.39
  210.6 12.3 %all_gather.37 = bf16[4,4,128,128]{3,2,1,0:T(8,128)(2,1)S(1)} all-gather(bf16[1,4,128,128]{3,2,1,0:T(8,128)(2,1)S(1)} %fusion.39), channel_id=1, replica_groups=mesh['seq_0'=4,'seq_1'=4,'seq_2'=2,'head'=8] {'seq_0'}, dimensions={0}, use_global_device_ids=true | all-gather | bytes 655360 | tf_op jit(solution)/shard_map/all_gather | solution.py:26
  222.9 0.3 fusion.29
  223.2 0.4 fusion.44
  223.6 0.0 copy-done.1
  223.7 0.0 copy-done.6
  223.7 0.6 fusion.2
  224.3 1.0 copy.49
  225.3 2.0 select_convert_fusion
  227.3 0.4 fusion.43
  227.7 0.0 copy-start.2
  227.7 1.4 fusion.1
  229.1 0.0 copy-start.4
  229.1 2.1 copy.48
  231.2 1.8 convolution_bitcast_fusion
  233.0 0.0 copy-done.2
  233.1 0.0 copy-done.4
  233.1 0.6 convolution_add_fusion.2
  233.7 0.3 copy.41
  234.0 0.9 multiply_convert_fusion.1
  234.9 42.5 %reduce-scatter.5.cloned.1.call-done = bf16[128,512]{1,0:T(8,128)(2,1)} async-done(((bf16[4096,512]{1,0:T(8,128)(2,1)}), bf16[128,512]{1,0:T(8,128)(2,1)}) %reduce-scatter.5.cloned.1.call-update) | async-done | bytes 131088 | tf_op jit(solution)/shard_map/reduce_scatter | solution.py:89
  277.4 1.6 convert_element_type.247
  (3 shorter events, 0.1 us)
Async XLA Ops:
  7.2 3.7 %copy-start = (bf16[512,512]{1,0:T(8,128)(2,1)S(1)}, bf16[512,512]{1,0:T(8,128)(2,1)}, u32[]{:S(2)}) copy-start(bf16[512,512]{1,0:T(8,128)(2,1)} %param.7) | copy-start | bytes 1572868
  7.2 56.7 %all-gather.5.cloned.1.call-start = ((), (), s32[]{:S(2)}) async-start(), calls=%async_computation.2 | async-start | bytes 4325376 | tf_op jit(solution)/shard_map/all_gather | solution.py:73
  7.9 118.7 %reduce-scatter.3.cloned.1.call-start = ((), (), s32[]{:S(2)}) async-start(), calls=%async_computation.3 | async-start | bytes 4718592 | tf_op jit(solution)/shard_map/reduce_scatter | solution.py:77
  9.2 31.0 %copy-start.5 = (bf16[512,512]{0,1:T(8,128)(2,1)}, bf16[512,512]{0,1:T(8,128)(2,1)S(1)}, u32[]{:S(2)}) copy-start(bf16[512,512]{0,1:T(8,128)(2,1)S(1)} %copy.82) | copy-start | bytes 1572868
  13.3 29.8 %copy-start.7 = (pred[512,512]{1,0:T(8,128)(4,1)}, pred[512,512]{1,0:T(8,128)(4,1)S(1)}, u32[]{:S(2)}) copy-start(pred[512,512]{1,0:T(8,128)(4,1)S(1)} %iota_compare_fusion) | copy-start | bytes 786436
  40.2 2.8 copy-start.3
  70.6 111.7 %all-gather.7.cloned.1.call-start = ((), (), s32[]{:S(2)}) async-start(), calls=%async_computation.4 | async-start | bytes 4718592 | tf_op jit(solution)/shard_map/all_gather | solution.py:81
  128.7 148.7 %reduce-scatter.5.cloned.1.call-start = ((), (), s32[]{:S(2)}) async-start(), calls=%async_computation.5 | async-start | bytes 4325376 | tf_op jit(solution)/shard_map/reduce_scatter | solution.py:89
  194.9 28.7 %copy-start.1 = (bf16[512,512]{0,1:T(8,128)(2,1)}, bf16[512,512]{0,1:T(8,128)(2,1)S(1)}, u32[]{:S(2)}) copy-start(bf16[512,512]{0,1:T(8,128)(2,1)S(1)} %convolution_convert_fusion.1) | copy-start | bytes 1572868
  195.3 28.4 %copy-start.6 = (bf16[512,512]{1,0:T(8,128)(2,1)S(1)}, bf16[512,512]{1,0:T(8,128)(2,1)}, u32[]{:S(2)}) copy-start(bf16[512,512]{1,0:T(8,128)(2,1)} %param.6) | copy-start | bytes 1572868
  227.7 5.3 %copy-start.2 = (bf16[512,512]{0,1:T(8,128)(2,1)S(1)}, bf16[512,512]{0,1:T(8,128)(2,1)}, u32[]{:S(2)}) copy-start(bf16[512,512]{0,1:T(8,128)(2,1)} %copy-done.1) | copy-start | bytes 1572868
  229.1 4.0 %copy-start.4 = (f32[4,128,128]{2,1,0:T(8,128)S(1)}, f32[4,128,128]{2,1,0:T(8,128)}, u32[]{:S(2)}) copy-start(f32[4,128,128]{2,1,0:T(8,128)} %copy-done.3) | copy-start | bytes 786436
Sparse Core Ops, SparseCore 0:
  10.5 53.2 all-gather.4
  70.8 55.7 reduce-scatter.2
  128.9 53.3 all-gather.6
  189.2 88.1 reduce-scatter.4
where the time goes:
time: 286 us
  waiting for transfers between devices  172 us (60%)
  blocking collectives  56.1 us (20%)
  matrix products  31.3 us (11%)
  between operations  14.1 us (5%)
  other arithmetic  6.88 us (2%)
  local copies, waits for them, and re-layouts  4.94 us (2%)
    all_gather x6, blocking collectives, entering(): pieces = lax.all_gather(so_far.astype(jnp.bfloat16), axis)  56.1 us
    reduce_scatter x1, waiting for transfers between devices, on_device(): lax.psum_scatter(partial_out.astype(jnp.bfloat16), 'head', scatter_dimens...  55.9 us
    all_gather x1, waiting for transfers between devices, on_device(): residual_full = lax.all_gather(residual, 'head', axis=1, tiled=True)  53.6 us
    reduce_scatter x1, waiting for transfers between devices, on_device(): lax.psum_scatter((product * weight_factor).astype(jnp.bfloat16), SEQ, sca...  42.5 us
    all_gather x1, waiting for transfers between devices, on_device(): whole_weight = lax.all_gather(out_weight, SEQ, axis=0, tiled=True)  19.4 us
    dot_general x1, matrix products, on_device(): lax.dot_general(attended, whole_weight, (((1,), (1,)), ((), ())), preferr...  6.73 us
    dot_general x1, matrix products, on_device(): lax.dot_general(residual_full, attended, (((0,), (0,)), ((), ())), prefer...  6.68 us
    dot_general x1, matrix products, on_device(): jnp.dot(residual_full, whole_weight, preferred_element_type=jnp.float32)  5.84 us
  transfers between devices with their start and end apart: 4, of which 4 were waited for; matrix products, arithmetic and copies ran while one was open for 9% of the time, Pallas kernels for 0%

commit v1 on v0

v1 whole, which is shorter than its diff:
```python
import math

import jax
import jax.numpy as jnp
from jax import lax
from jax.experimental import pallas as pl
from jax.experimental.pallas import tpu as pltpu
from jax.sharding import Mesh
from jax.sharding import PartitionSpec as P

DH = 128
ROWS = 512
HEADS = 4
SEQ = ("seq_0", "seq_1", "seq_2")
MESH = pl.DeviceIdType.MESH
F32 = jnp.float32
BF16 = jnp.bfloat16
NT = (((1,), (1,)), ((), ()))
NN = (((1,), (0,)), ((), ()))
TN = (((0,), (0,)), ((), ()))
UP_ORDER = (2, 3, 0, 1)
DOWN_ORDER = (0, 1, 2, 3)
GATHER_ORDER = (0, 2, 1, 3)


def dot(a, b, dims):
    return lax.dot_general(a, b, dims, preferred_element_type=F32)


def remote(src, dst, send, recv, **device):
    return pltpu.make_async_remote_copy(
        src_ref=src, dst_ref=dst, send_sem=send, recv_sem=recv, device_id=device, device_id_type=MESH
    )


def wait_bytes(ref, sem):
    pltpu.make_async_copy(ref, ref, sem).wait()


def kernel(
    weight_factor,
    q_in, k_in, v_in, w_in, t_in,
    out_o, gq_o, gk_o, gv_o, gw_o,
    qb, kb, vb, tb, scaled, wf, att, pb, su, sd, ru, rd, res, da, dab, dw, cw, xs, xr, ysend, yown, yrecv,
    scores, gk_acc, gv_acc, oq, ok, ov,
    tot, loc, sib, ct, xrc, rt, yrc, pfs, pfr, px, state,
    in_sem, out_sem, rs_recv, ag_recv, z_send, w_recv, w_send, sc_recv, sc_send, d_recv, d_send,
):
    y = lax.axis_index("seq_0")
    x = lax.axis_index("seq_1")
    c = lax.axis_index("seq_2")
    z = lax.axis_index("head")
    up = lax.rem(z + 1, 8)
    down = lax.rem(z + 7, 8)
    sibling = 1 - c
    half = lax.div(z, 2)
    turn = 2 * lax.rem(z, 2) - 1

    def block(k):
        return lax.rem(z + k + 8, 8)

    def level_row(level):
        shift = {1: 0, 2: turn, 3: -turn, 4: 2}[level]
        return lax.rem(half + shift + 4, 4)

    loads = [
        pltpu.make_async_copy(w_in, wf.at[y, x, c], in_sem.at[0]),
        pltpu.make_async_copy(k_in, kb, in_sem.at[1]),
        pltpu.make_async_copy(v_in, vb, in_sem.at[2]),
        pltpu.make_async_copy(q_in, qb, in_sem.at[3]),
        pltpu.make_async_copy(t_in, tb, in_sem.at[4]),
    ]
    for copy in loads:
        copy.start()

    barrier = pltpu.get_barrier_semaphore()
    partners = [{"head": up}, {"head": down}, {"seq_2": sibling}]
    partners += [{"seq_1": lax.rem(x + d, 4)} for d in (1, 2, 3)]
    partners += [{"seq_0": lax.rem(y + d, 4)} for d in (1, 2, 3)]
    for partner in partners:
        pl.semaphore_signal(barrier, inc=1, device_id=partner, device_id_type=MESH)
    pl.semaphore_wait(barrier, len(partners))

    loads[0].wait()
    for d in (1, 3, 2):
        remote(
            wf.at[y, x, c], wf.at[y, x, c], w_send.at[0], w_recv.at[d - 1], seq_0=lax.rem(y + d, 4)
        ).start()

    def head_columns(h):
        return pl.ds(pl.multiple_of(h * DH, DH), DH)

    def scan_begin(n):
        loc[n] = tot[n].astype(BF16)
        remote(loc.at[n], sib.at[n], sc_send.at[n, 0], sc_recv.at[n, 0], seq_2=sibling).start()

    mine = pl.ds(2 * c, 2)

    def scan_x(n):
        remote(sib.at[n], sib.at[n], sc_send.at[n, 0], sc_recv.at[n, 0], seq_2=sibling).wait_recv()
        chip = tot[n, mine] + sib[n, mine].astype(F32)
        ct[n] = chip.astype(BF16)
        for d in (1, 3, 2):
            remote(
                ct.at[n], xrc.at[n, d - 1], sc_send.at[n, 1], sc_recv.at[n, d], seq_1=lax.rem(x + d, 4)
            ).start()

    def scan_y(n, reverse):
        total = ct[n].astype(F32)
        passed = jnp.zeros((2, DH, DH), F32)
        for d in (1, 3, 2):
            remote(
                ct.at[n], xrc.at[n, d - 1], sc_send.at[n, 1], sc_recv.at[n, d], seq_1=lax.rem(x + d, 4)
            ).wait_recv()
            piece = xrc[n, d - 1].astype(F32)
            total = total + piece
            counts = (d > x) if reverse else (d <= x)
            passed = passed + piece * counts.astype(F32)
        rt[n] = total.astype(BF16)
        px[n] = passed
        for d in (1, 3, 2):
            remote(
                rt.at[n], yrc.at[n, d - 1], sc_send.at[n, 2], sc_recv.at[n, 3 + d], seq_0=lax.rem(y + d, 4)
            ).start()

    def scan_core(n, reverse):
        passed = px[n]
        for d in (1, 3, 2):
            remote(
                rt.at[n], yrc.at[n, d - 1], sc_send.at[n, 2], sc_recv.at[n, 3 + d], seq_0=lax.rem(y + d, 4)
            ).wait_recv()
            counts = (d > y) if reverse else (d <= y)
            passed = passed + yrc[n, d - 1].astype(F32) * counts.astype(F32)
        px[n] = passed
        pfs[n] = passed.astype(BF16)
        remote(pfs.at[n], pfr.at[n], sc_send.at[n, 3], sc_recv.at[n, 7], seq_2=sibling).start()

    def scan_end(n, reverse):
        remote(pfs.at[n], pfr.at[n], sc_send.at[n, 3], sc_recv.at[n, 7], seq_2=sibling).wait_recv()
        own_core = (c == 0) if reverse else (c == 1)
        factor = own_core.astype(F32)
        theirs = pl.ds(2 * sibling, 2)
        state[n, mine] = (px[n] + sib[n, mine].astype(F32) * factor).astype(BF16)
        state[n, theirs] = (pfr[n].astype(F32) + sib[n, theirs].astype(F32) * factor).astype(BF16)

    loads[1].wait()
    loads[2].wait()

    @pl.loop(0, HEADS)
    def _(h):
        cols = head_columns(h)
        tot[0, h] = dot(kb[:, cols], vb[:, cols], TN)

    scan_begin(0)
    first = lax.rem((y * 4 + x) * 2 + c, 32) * ROWS
    positions = (first + lax.broadcasted_iota(jnp.int32, (ROWS, 1), 0) + 1).astype(F32)
    scale = lax.rsqrt(F32(DH) * positions)
    loads[3].wait()
    scaled[...] = (qb[...].astype(F32) * scale).astype(BF16)
    scan_x(0)

    causal = lax.broadcasted_iota(jnp.int32, (ROWS, ROWS), 0) >= lax.broadcasted_iota(
        jnp.int32, (ROWS, ROWS), 1
    )

    for d in (1, 3, 2):
        src = lax.rem(y + 4 - d, 4)
        remote(
            wf.at[src, x, c], wf.at[src, x, c], w_send.at[0], w_recv.at[d - 1], seq_0=lax.rem(y + d, 4)
        ).wait_recv()

    def weight_x(level):
        row = level_row(level)
        for d in (1, 3, 2):
            remote(
                wf.at[row, x, c],
                wf.at[row, x, c],
                w_send.at[1],
                w_recv.at[3 + 3 * (level - 1) + d - 1],
                seq_1=lax.rem(x + d, 4),
            ).start()

    def weight_core(level):
        row = level_row(level)
        for d in (1, 3, 2):
            src = lax.rem(x + 4 - d, 4)
            remote(
                wf.at[row, src, c],
                wf.at[row, src, c],
                w_send.at[1],
                w_recv.at[3 + 3 * (level - 1) + d - 1],
                seq_1=lax.rem(x + d, 4),
            ).wait_recv()
        remote(
            wf.at[row, :, c], wf.at[row, :, c], w_send.at[2], w_recv.at[14 + level], seq_2=sibling
        ).start()

    def weight_ready(level):
        row = level_row(level)
        remote(
            wf.at[row, :, sibling], wf.at[row, :, sibling], w_send.at[2], w_recv.at[14 + level], seq_2=sibling
        ).wait_recv()

    for level in (4, 3, 2, 1):
        weight_x(level)

    @pl.loop(0, HEADS)
    def _(h):
        cols = head_columns(h)
        s = dot(scaled[:, cols], kb[:, cols], NT)
        scores[h] = jnp.where(causal, s, 0.0).astype(BF16)

    scan_y(0, False)

    @pl.loop(0, HEADS)
    def _(h):
        cols = head_columns(h)
        gk_acc[:, cols] = dot(scores[h], vb[:, cols], NN)

    weight_core(4)
    scan_core(0, False)
    scan_end(0, False)

    @pl.loop(0, HEADS)
    def _(h):
        cols = head_columns(h)
        att[:, cols] = (dot(scaled[:, cols], state[0, h], NN) + gk_acc[:, cols]).astype(BF16)

    def weight_block(b):
        w = wf[lax.div(b, 2), pl.ds(2 * lax.rem(b, 2), 2)]
        return w.reshape(ROWS, ROWS)

    def partial(u, b):
        pb[u] = dot(att[...], weight_block(b), NT).reshape(4, 128, ROWS)

    def reduce_copy(u, idx):
        src, dst = (su, ru) if u == 0 else (sd, rd)
        return remote(
            src.at[idx], dst.at[idx], z_send.at[u], rs_recv.at[u, idx], head=up if u == 0 else down
        )

    def reduce_send(u, idx, r, received):
        src, dst = (su, ru) if u == 0 else (sd, rd)
        value = pb[u, r]
        if received is not None:
            reduce_copy(u, received).wait_recv()
            value = value + dst[received].astype(F32)
        src[idx] = value.astype(BF16)
        reduce_copy(u, idx).start()

    weight_ready(4)
    partial(0, block(4))
    pb[1] = pb[0]
    for i in (0, 1):
        reduce_send(0, i, i, None)
        reduce_send(1, i, 2 + i, None)
    weight_core(3)
    weight_ready(3)
    partial(0, block(3))
    partial(1, block(-3))
    for j in range(4):
        reduce_send(0, 2 + j, UP_ORDER[j], None if j < 2 else j - 2)
        reduce_send(1, 2 + j, DOWN_ORDER[j], None if j < 2 else j - 2)
    for k in (2, 1):
        weight_core(k)
        weight_ready(k)
        partial(0, block(k))
        partial(1, block(-k))
        for j in range(4):
            idx = 4 * (3 - k) + 2 + j
            reduce_send(0, idx, UP_ORDER[j], idx - 4)
            reduce_send(1, idx, DOWN_ORDER[j], idx - 4)
    partial(0, z)

    def gather_copy(u, idx, b, r):
        return remote(
            res.at[b, r], res.at[b, r], z_send.at[2 + u], ag_recv.at[u, idx], head=up if u == 0 else down
        )

    loads[4].wait()
    for j, r in enumerate(GATHER_ORDER):
        i_up = 10 + UP_ORDER.index(r)
        i_down = 10 + DOWN_ORDER.index(r)
        reduce_copy(0, i_up).wait_recv()
        reduce_copy(1, i_down).wait_recv()
        value = (pb[0, r] + ru[i_up].astype(F32) + rd[i_down].astype(F32)).astype(BF16)
        rows = pl.ds(r * 128, 128)
        ov[rows, :] = value
        res[z, r] = (value.astype(F32) - tb[rows, :].astype(F32)).astype(BF16)
        gather_copy(0, j, z, r).start()
        gather_copy(1, j, z, r).start()
    out_copy = pltpu.make_async_copy(ov, out_o, out_sem.at[0])
    out_copy.start()

    def grads(b, begin=False):
        r_b = res[b].reshape(ROWS, ROWS)
        term = dot(r_b, weight_block(b), NN)
        da[...] = term if begin else da[...] + term

    def weight_grads(b):
        r_b = res[b].reshape(ROWS, ROWS)
        d_b = dot(r_b, att[...], TN).astype(BF16)
        dw[lax.div(b, 2), pl.ds(2 * lax.rem(b, 2), 2)] = d_b.reshape(2, 2, 128, ROWS)

    def dw_core(level):
        row = level_row(level)
        remote(
            dw.at[row, :, sibling], cw.at[level - 1], d_send.at[0], d_recv.at[level - 1], seq_2=sibling
        ).start()

    def dw_x(level):
        row = level_row(level)
        remote(
            cw.at[level - 1], cw.at[level - 1], d_send.at[0], d_recv.at[level - 1], seq_2=sibling
        ).wait_recv()
        for d in (1, 3, 2, 0):
            to = lax.rem(x + d, 4)
            xs[level - 1, to] = (
                dw[row, to, c].astype(F32) + cw[level - 1, to].astype(F32)
            ).astype(BF16)
            if d:
                remote(
                    xs.at[level - 1, to],
                    xr.at[level - 1, d - 1],
                    d_send.at[1],
                    d_recv.at[4 + 3 * (level - 1) + d - 1],
                    seq_1=to,
                ).start()

    def dw_y(level):
        row = level_row(level)
        total = xs[level - 1, x].astype(F32)
        for d in (1, 3, 2):
            remote(
                xr.at[level - 1, d - 1],
                xr.at[level - 1, d - 1],
                d_send.at[1],
                d_recv.at[4 + 3 * (level - 1) + d - 1],
                seq_1=lax.rem(x + d, 4),
            ).wait_recv()
            total = total + xr[level - 1, d - 1].astype(F32)

        @pl.when(row == y)
        def _():
            yown[...] = total

        @pl.when(row != y)
        def _():
            ysend[level - 1] = total.astype(BF16)
            d = lax.rem(row - y + 4, 4)
            remote(
                ysend.at[level - 1], yrecv.at[d - 1], d_send.at[2], d_recv.at[16 + d - 1], seq_0=row
            ).start()

    grads(z, begin=True)
    weight_grads(z)
    for k in (1, 2, 3):
        for j, r in enumerate(GATHER_ORDER):
            for u in (0, 1):
                b = block(-k if u == 0 else k)
                gather_copy(u, 4 * (k - 1) + j, b, r).wait_recv()
                if k < 3:
                    gather_copy(u, 4 * k + j, b, r).start()
                elif u == 0 and j < 2:
                    gather_copy(u, 12 + j, b, r).start()
                elif u == 1 and j >= 2:
                    gather_copy(u, 12 + j - 2, b, r).start()

        @pl.loop(0, 2)
        def _(u, k=k):
            b = block(k * (2 * u - 1))
            grads(b)
            weight_grads(b)

        dw_core(k)
        if k >= 2:
            dw_x(k - 1)
        if k >= 3:
            dw_y(k - 2)

    b4 = block(4)
    for i in (0, 1):
        gather_copy(0, 12 + i, b4, GATHER_ORDER[i]).wait_recv()
        gather_copy(1, 12 + i, b4, GATHER_ORDER[2 + i]).wait_recv()
    grads(b4)
    dab[...] = da[...].astype(BF16)

    @pl.loop(0, HEADS)
    def _(h):
        cols = head_columns(h)
        tot[1, h] = dot(scaled[:, cols], dab[:, cols], TN)

    scan_begin(1)
    weight_grads(b4)
    dw_core(4)
    scan_x(1)
    dw_x(3)
    dw_x(4)

    @pl.loop(0, HEADS)
    def _(h):
        cols = head_columns(h)
        mixed = jnp.where(causal, dot(dab[:, cols], vb[:, cols], NT), 0.0).astype(BF16)
        g = dot(dab[:, cols], state[0, h], NT) + dot(mixed, kb[:, cols], NN)
        oq[:, cols] = (g * scale).astype(BF16)
        gk_acc[:, cols] = dot(mixed, scaled[:, cols], TN)
        gv_acc[:, cols] = dot(scores[h], dab[:, cols], TN)

    scan_y(1, True)
    q_copy = pltpu.make_async_copy(oq, gq_o, out_sem.at[1])
    q_copy.start()
    dw_y(2)
    dw_y(3)
    scan_core(1, True)
    dw_y(4)
    scan_end(1, True)
    out_copy.wait()

    @pl.loop(0, HEADS)
    def _(h):
        cols = head_columns(h)
        ok[:, cols] = (gk_acc[:, cols] + dot(vb[:, cols], state[1, h], NT)).astype(BF16)
        ov[:, cols] = (gv_acc[:, cols] + dot(kb[:, cols], state[1, h], NN)).astype(BF16)

    k_copy = pltpu.make_async_copy(ok, gk_o, out_sem.at[2])
    k_copy.start()
    v_copy = pltpu.make_async_copy(ov, gv_o, out_sem.at[3])
    v_copy.start()
    total = yown[...]
    for d in (1, 3, 2):
        remote(
            yrecv.at[d - 1], yrecv.at[d - 1], d_send.at[2], d_recv.at[16 + d - 1], seq_0=lax.rem(y + d, 4)
        ).wait_recv()
        total = total + yrecv[d - 1].astype(F32)
    yown[...] = total * weight_factor
    w_copy = pltpu.make_async_copy(yown, gw_o, out_sem.at[4])
    w_copy.start()

    wait_bytes(su, z_send.at[0])
    wait_bytes(sd, z_send.at[1])
    wait_bytes(su, z_send.at[2])
    wait_bytes(sd, z_send.at[3])
    wait_bytes(xr.at[0], w_send.at[0])
    wait_bytes(xr, w_send.at[1])
    wait_bytes(xs, w_send.at[2])
    wait_bytes(cw, d_send.at[0])
    wait_bytes(xr, d_send.at[1])
    wait_bytes(yrecv, d_send.at[2])
    for n in (0, 1):
        wait_bytes(loc.at[n], sc_send.at[n, 0])
        wait_bytes(xrc.at[n], sc_send.at[n, 1])
        wait_bytes(yrc.at[n], sc_send.at[n, 2])
        wait_bytes(pfs.at[n], sc_send.at[n, 3])
    for copy in (q_copy, k_copy, v_copy, w_copy):
        copy.wait()


def on_device(query_rows, key_rows, value_rows, out_weight, target_rows):
    rows = jax.ShapeDtypeStruct((ROWS, ROWS), BF16)
    total_rows = query_rows.shape[0] * lax.axis_size(SEQ)
    full = (ROWS, ROWS)
    vm = pltpu.VMEM
    scratch = (
        [vm(full, BF16)] * 5
        + [
            vm((4, 4, 2, 128, ROWS), BF16),
            vm(full, BF16),
            vm((2, 4, 128, ROWS), F32),
        ]
        + [vm((14, 128, ROWS), BF16)] * 4
        + [
            vm((8, 4, 128, ROWS), BF16),
            vm(full, F32),
            vm(full, BF16),
            vm((4, 4, 2, 128, ROWS), BF16),
            vm((4, 4, 128, ROWS), BF16),
            vm((4, 4, 128, ROWS), BF16),
            vm((4, 3, 128, ROWS), BF16),
            vm((4, 128, ROWS), BF16),
            vm((128, ROWS), F32),
            vm((3, 128, ROWS), BF16),
            vm((HEADS, ROWS, ROWS), BF16),
            vm(full, F32),
            vm(full, F32),
        ]
        + [vm(full, BF16)] * 3
        + [
            vm((2, HEADS, DH, DH), F32),
            vm((2, HEADS, DH, DH), BF16),
            vm((2, HEADS, DH, DH), BF16),
            vm((2, 2, DH, DH), BF16),
            vm((2, 3, 2, DH, DH), BF16),
            vm((2, 2, DH, DH), BF16),
            vm((2, 3, 2, DH, DH), BF16),
            vm((2, 2, DH, DH), BF16),
            vm((2, 2, DH, DH), BF16),
            vm((2, 2, DH, DH), F32),
            vm((2, HEADS, DH, DH), BF16),
        ]
    )
    dma = pltpu.SemaphoreType.DMA
    scratch += [
        dma((5,)), dma((5,)), dma((2, 14)), dma((2, 14)), dma((4,)), dma((19,)), dma((3,)),
        dma((2, 8)), dma((2, 4)), dma((19,)), dma((3,)),
    ]
    anywhere = pl.BlockSpec(memory_space=pl.ANY)

    def body(*refs):
        kernel(1.0 / math.sqrt(total_rows), *refs)

    return pl.pallas_call(
        body,
        out_shape=(rows, rows, rows, rows, jax.ShapeDtypeStruct((128, ROWS), F32)),
        in_specs=[anywhere] * 5,
        out_specs=(anywhere,) * 5,
        scratch_shapes=scratch,
        compiler_params=pltpu.CompilerParams(
            collective_id=0, has_side_effects=True, vmem_limit_bytes=60 * 1024 * 1024
        ),
        name="linear_attention",
    )(query_rows, key_rows, value_rows, out_weight, target_rows)


def solution(mesh):
    torus = Mesh(
        mesh.devices.reshape(4, 4, 2, mesh.shape["head"]), ("seq_0", "seq_1", "seq_2", "head")
    )
    spec = P(SEQ, "head")
    return jax.shard_map(
        on_device, mesh=torus, in_specs=(spec,) * 5, out_specs=(spec,) * 5, check_vma=False
    )
```

time: 286 us -> 142 us (0.50)
  waiting for transfers between devices: 172 us -> 0 us
  Pallas kernels: 0 us -> 135 us
  blocking collectives: 56.1 us -> 0 us
  matrix products: 31.3 us -> 0 us
  between operations: 14.1 us -> 0.65 us
  other arithmetic: 6.88 us -> 0 us
    pallas_call x0 -> x1, Pallas kernels: none -> 135 us  [on_device(): pl.pallas_call(body, out_shape=(rows, rows, rows, rows, jax.ShapeDtypeStr...]
    reduce_scatter x2 -> x0, waiting for transfers between devices: 98.4 us -> none  [the longest x1 55.9 us: on_device(): lax.psum_scatter(partial_out.astype(jnp.bfloat16), 'head', scatter_dimens...]
    all_gather x2 -> x0, waiting for transfers between devices: 73 us -> none  [the longest x1 53.6 us: on_device(): residual_full = lax.all_gather(residual, 'head', axis=1, tiled=True)]
    all_gather x6 -> x0, blocking collectives: 56.1 us -> none  [entering(): pieces = lax.all_gather(so_far.astype(jnp.bfloat16), axis)]
    dot_general x15 -> x0, matrix products: 31.3 us -> none  [the longest x1 6.73 us: on_device(): lax.dot_general(attended, whole_weight, (((1,), (1,)), ((), ())), preferr...]
    convert_element_type x8 -> x0, other arithmetic: 6.29 us -> none  [the longest x1 2.12 us: on_device(): (summed.astype(jnp.float32) - target_rows.astype(jnp.float32)).astype(jnp...]
    unnamed x18 -> x13, local copies, waits for them, and re-layouts: 3.14 us -> 6.18 us
  transfers between devices with their start and end apart: 4 -> 0, of which waited for: 4 -> 0; matrix products, arithmetic and copies ran while one was open for 9% -> 0% of each run, Pallas kernels for 0% -> 0%
where the time goes in v1:
time: 142 us
  Pallas kernels  135 us (95%)
  local copies, waits for them, and re-layouts  6.18 us (4%)
    pallas_call x1, Pallas kernels, on_device(): pl.pallas_call(body, out_shape=(rows, rows, rows, rows, jax.ShapeDtypeStr...  135 us
    unnamed x13, local copies, waits for them, and re-layouts  6.18 us

profile of v1, /device:TPU:16, one launch (start us, length us, event | category | flops | bytes accessed | tf_op | source)
XLA Modules:
  0.0 141.9 jit_solution(16240936385096213245)
XLA Ops:
  0.6 135.0 %linear_attention.1 = (bf16[512,512]{1,0:T(8,128)(2,1)}, bf16[512,512]{1,0:T(8,128)(2,1)}, bf16[512,512]{1,0:T(8,128)(2,1)}, bf16[512,512]{1,0:T(8,128)(2,1)}, f32[128,512]{1,0:T(8,128)}) custom-call(bf16[512,512]{1,0:T(8,128)(2,1)} %refs_0_.1, bf16[512,512]{1,0:T(8,128)(2,1)} %refs_1_.1, bf16[512,512]{1,0:T(8,128)(2,1)} %refs_2_.1, ...), custom_call_target="tpu_custom_call" | custom-call | tf_op jit(solution)/shard_map/linear_attention/pallas_call | solution.py:511
  135.7 0.0 copy-start.2
  135.7 1.9 %copy.15 = bf16[512,512]{1,0:T(8,128)(2,1)} copy(bf16[512,512]{1,0:T(8,128)(2,1)} %get-tuple-element.10) | data formatting | bytes 1048576
  137.6 0.0 copy-done.2
  137.6 0.0 copy-start.1
  137.6 0.8 copy.16
  138.4 0.4 copy-done.1
  138.8 0.0 copy-start
  138.8 0.8 copy.17
  139.6 0.4 copy-done
  140.1 0.0 copy-start.3
  140.1 0.8 copy.18
  140.9 0.3 copy-done.3
  141.2 0.7 copy.19
Async XLA Ops:
  135.7 1.9 %copy-start.2 = (bf16[512,512]{1,0:T(8,128)(2,1)S(1)}, bf16[512,512]{1,0:T(8,128)(2,1)}, u32[]{:S(2)}) copy-start(bf16[512,512]{1,0:T(8,128)(2,1)} %get-tuple-element.11) | copy-start | bytes 1572868
  137.6 1.2 copy-start.1
  138.8 1.2 copy-start
  140.1 1.1 copy-start.3

commit v2 on v1

v2 whole, which is shorter than its diff:
```python
import math

import jax
import jax.numpy as jnp
from jax import lax
from jax.experimental import pallas as pl
from jax.experimental.pallas import tpu as pltpu
from jax.sharding import Mesh
from jax.sharding import PartitionSpec as P

DH = 128
ROWS = 512
HEADS = 4
SEQ = ("seq_0", "seq_1", "seq_2")
MESH = pl.DeviceIdType.MESH
F32 = jnp.float32
BF16 = jnp.bfloat16
NT = (((1,), (1,)), ((), ()))
NN = (((1,), (0,)), ((), ()))
TN = (((0,), (0,)), ((), ()))


def dot(a, b, dims):
    return lax.dot_general(a, b, dims, preferred_element_type=F32)


def remote(src, dst, send, recv, **device):
    return pltpu.make_async_remote_copy(
        src_ref=src, dst_ref=dst, send_sem=send, recv_sem=recv, device_id=device, device_id_type=MESH
    )


def wait_bytes(ref, sem):
    pltpu.make_async_copy(ref, ref, sem).wait()


def kernel(
    weight_factor,
    q_in, k_in, v_in, w_in, t_in,
    out_o, gq_o, gk_o, gv_o, gw_o,
    qb, kb, vb, tb, scaled, wf, att, pb, su, sd, ru, rd, res, da, dab, dw, cw, xs, xh, xr, ysend, yown, yrecv,
    scores, gk_acc, gv_acc, oq, ok, ov,
    tot, loc, sib, ct, xrc, rt, yrc, pfs, pfr, px, state,
    in_sem, out_sem, rs_recv, ag_recv, z_send, wy_recv, wx_recv, wc_recv, w_send, sc_recv, sc_send,
    dc_recv, dx_recv, dy_recv, d_send,
):
    y = lax.axis_index("seq_0")
    x = lax.axis_index("seq_1")
    c = lax.axis_index("seq_2")
    z = lax.axis_index("head")
    up = lax.rem(z + 1, 8)
    down = lax.rem(z + 7, 8)
    sibling = 1 - c
    right = lax.rem(x + 1, 4)
    left = lax.rem(x + 3, 4)
    across = lax.rem(x + 2, 4)
    half = lax.div(z, 2)
    turn = 2 * lax.rem(z, 2) - 1
    first_half = pl.ds(0, 64)
    second_half = pl.ds(64, 64)

    def block(k):
        return lax.rem(z + k + 8, 8)

    def level_row(level):
        shift = {1: 0, 2: turn, 3: -turn, 4: 2}[level]
        return lax.rem(half + shift + 4, 4)

    loads = [
        pltpu.make_async_copy(w_in, wf.at[y, x, c], in_sem.at[0]),
        pltpu.make_async_copy(k_in, kb, in_sem.at[1]),
        pltpu.make_async_copy(v_in, vb, in_sem.at[2]),
        pltpu.make_async_copy(q_in, qb, in_sem.at[3]),
        pltpu.make_async_copy(t_in, tb, in_sem.at[4]),
    ]
    for copy in loads:
        copy.start()

    barrier = pltpu.get_barrier_semaphore()
    partners = [{"head": up}, {"head": down}, {"seq_2": sibling}]
    partners += [{"seq_1": lax.rem(x + d, 4)} for d in (1, 2, 3)]
    partners += [{"seq_0": lax.rem(y + d, 4)} for d in (1, 2, 3)]
    for partner in partners:
        pl.semaphore_signal(barrier, inc=1, device_id=partner, device_id_type=MESH)
    pl.semaphore_wait(barrier, len(partners))

    def weight_y():
        for d in (2, 3, 1):
            remote(
                wf.at[y, x, c], wf.at[y, x, c], w_send.at[0], wy_recv.at[d - 1], seq_0=lax.rem(y + d, 4)
            ).start()

    def weight_to_core(row, col, slot):
        return remote(
            wf.at[row, col, c], wf.at[row, col, c], w_send.at[2], wc_recv.at[slot], seq_2=sibling
        )

    def weight_side(level, toward_right, whole):
        row = level_row(level)
        to, source = (right, left) if toward_right else (left, right)
        slot = 4 * (level - 1) + (0 if toward_right else 1) + (0 if whole else 2)
        sem = wx_recv.at[slot]
        if whole:
            sent, got = wf.at[row, x, c], wf.at[row, source, c]
        else:
            part = first_half if toward_right else second_half
            sent, got = wf.at[row, source, c, part], wf.at[row, across, c, part]
        return (
            lambda: remote(sent, sent, w_send.at[1], sem, seq_1=to).start(),
            lambda: remote(got, got, w_send.at[1], sem, seq_1=to).wait_recv(),
        )

    def weight_1(level):
        row = level_row(level)

        @pl.when(row != y)
        def _():
            d = lax.rem(y - row + 4, 4)
            remote(
                wf.at[row, x, c], wf.at[row, x, c], w_send.at[0], wy_recv.at[d - 1], seq_0=row
            ).wait_recv()

        weight_side(level, True, True)[0]()
        weight_side(level, False, True)[0]()
        weight_to_core(row, x, 4 * (level - 1)).start()

    def weight_2(level):
        row = level_row(level)
        for i, toward_right in enumerate((True, False)):
            weight_side(level, toward_right, True)[1]()
            weight_side(level, toward_right, False)[0]()
            weight_to_core(row, left if toward_right else right, 4 * (level - 1) + 1 + i).start()

    def weight_3(level):
        row = level_row(level)
        for toward_right in (True, False):
            weight_side(level, toward_right, False)[1]()
        weight_to_core(row, across, 4 * (level - 1) + 3).start()

    def weight_ready(level):
        row = level_row(level)
        for i, col in enumerate((x, left, right, across)):
            slot = 4 * (level - 1) + i
            remote(
                wf.at[row, col, sibling], wf.at[row, col, sibling], w_send.at[2], wc_recv.at[slot],
                seq_2=sibling,
            ).wait_recv()

    loads[0].wait()

    @pl.when(level_row(4) == y)
    def _():
        weight_y()

    def head_columns(h):
        return pl.ds(pl.multiple_of(h * DH, DH), DH)

    def scan_begin(n):
        loc[n] = tot[n].astype(BF16)
        remote(loc.at[n], sib.at[n], sc_send.at[n, 0], sc_recv.at[n, 0], seq_2=sibling).start()

    mine = pl.ds(2 * c, 2)

    def scan_x(n):
        remote(sib.at[n], sib.at[n], sc_send.at[n, 0], sc_recv.at[n, 0], seq_2=sibling).wait_recv()
        chip = tot[n, mine] + sib[n, mine].astype(F32)
        ct[n] = chip.astype(BF16)
        for d in (2, 1, 3):
            remote(
                ct.at[n], xrc.at[n, d - 1], sc_send.at[n, 1], sc_recv.at[n, d], seq_1=lax.rem(x + d, 4)
            ).start()

    def scan_y(n, reverse):
        total = ct[n].astype(F32)
        passed = jnp.zeros((2, DH, DH), F32)
        for d in (1, 3, 2):
            remote(
                ct.at[n], xrc.at[n, d - 1], sc_send.at[n, 1], sc_recv.at[n, d], seq_1=lax.rem(x + d, 4)
            ).wait_recv()
            piece = xrc[n, d - 1].astype(F32)
            total = total + piece
            counts = (d > x) if reverse else (d <= x)
            passed = passed + piece * counts.astype(F32)
        rt[n] = total.astype(BF16)
        px[n] = passed
        for d in (2, 1, 3):
            remote(
                rt.at[n], yrc.at[n, d - 1], sc_send.at[n, 2], sc_recv.at[n, 3 + d], seq_0=lax.rem(y + d, 4)
            ).start()

    def scan_core(n, reverse):
        passed = px[n]
        for d in (1, 3, 2):
            remote(
                rt.at[n], yrc.at[n, d - 1], sc_send.at[n, 2], sc_recv.at[n, 3 + d], seq_0=lax.rem(y + d, 4)
            ).wait_recv()
            counts = (d > y) if reverse else (d <= y)
            passed = passed + yrc[n, d - 1].astype(F32) * counts.astype(F32)
        px[n] = passed
        pfs[n] = passed.astype(BF16)
        remote(pfs.at[n], pfr.at[n], sc_send.at[n, 3], sc_recv.at[n, 7], seq_2=sibling).start()

    def scan_end(n, reverse):
        remote(pfs.at[n], pfr.at[n], sc_send.at[n, 3], sc_recv.at[n, 7], seq_2=sibling).wait_recv()
        own_core = (c == 0) if reverse else (c == 1)
        factor = own_core.astype(F32)
        theirs = pl.ds(2 * sibling, 2)
        state[n, mine] = (px[n] + sib[n, mine].astype(F32) * factor).astype(BF16)
        state[n, theirs] = (pfr[n].astype(F32) + sib[n, theirs].astype(F32) * factor).astype(BF16)

    loads[1].wait()
    loads[2].wait()

    @pl.loop(0, HEADS)
    def _(h):
        cols = head_columns(h)
        tot[0, h] = dot(kb[:, cols], vb[:, cols], TN)

    scan_begin(0)

    @pl.when(level_row(3) == y)
    def _():
        weight_y()

    first = lax.rem((y * 4 + x) * 2 + c, 32) * ROWS
    positions = (first + lax.broadcasted_iota(jnp.int32, (ROWS, 1), 0) + 1).astype(F32)
    scale = lax.rsqrt(F32(DH) * positions)
    loads[3].wait()
    scaled[...] = (qb[...].astype(F32) * scale).astype(BF16)
    scan_x(0)

    causal = lax.broadcasted_iota(jnp.int32, (ROWS, ROWS), 0) >= lax.broadcasted_iota(
        jnp.int32, (ROWS, ROWS), 1
    )

    @pl.loop(0, HEADS)
    def _(h):
        cols = head_columns(h)
        s = dot(scaled[:, cols], kb[:, cols], NT)
        scores[h] = jnp.where(causal, s, 0.0).astype(BF16)

    weight_1(4)

    @pl.loop(0, HEADS)
    def _(h):
        cols = head_columns(h)
        gk_acc[:, cols] = dot(scores[h], vb[:, cols], NN)

    scan_y(0, False)

    @pl.when(jnp.logical_and(level_row(4) != y, level_row(3) != y))
    def _():
        weight_y()

    weight_2(4)
    weight_1(3)
    scan_core(0, False)
    weight_3(4)
    scan_end(0, False)

    @pl.loop(0, HEADS)
    def _(h):
        cols = head_columns(h)
        att[:, cols] = (dot(scaled[:, cols], state[0, h], NN) + gk_acc[:, cols]).astype(BF16)

    up_order = (2 + c, 3 - c, c, 1 - c)
    down_order = (c, 1 - c, 2 + c, 3 - c)
    gather_order = (c, 2 + c, 1 - c, 3 - c)

    def block_cols(b):
        return lax.div(b, 2), pl.ds(2 * lax.rem(b, 2), 2)

    def weight_block(b):
        row, cols = block_cols(b)
        return wf[row, cols].reshape(ROWS, ROWS)

    def partial(u, b):
        value = dot(att[...], weight_block(b), NT)
        for r in range(4):
            pb[u, r] = value[:, r * 128 : (r + 1) * 128]

    def reduce_copy(u, idx):
        src, dst = (su, ru) if u == 0 else (sd, rd)
        return remote(
            src.at[idx], dst.at[idx], z_send.at[u], rs_recv.at[u, idx], head=up if u == 0 else down
        )

    def reduce_send(u, idx, r, received):
        src, dst = (su, ru) if u == 0 else (sd, rd)
        value = pb[u, r]
        if received is not None:
            reduce_copy(u, received).wait_recv()
            value = value + dst[received].astype(F32)
        src[idx] = value.astype(BF16)
        reduce_copy(u, idx).start()

    row4, cols4 = block_cols(block(4))
    for i, core in enumerate((c, sibling)):
        if i == 1:
            weight_ready(4)
        value = dot(att[...], wf[row4, cols4, core].reshape(256, ROWS), NT)
        su[i] = value[:, 0:128].astype(BF16)
        sd[i] = value[:, 128:256].astype(BF16)
        reduce_copy(0, i).start()
        reduce_copy(1, i).start()
    weight_2(3)
    weight_1(2)
    weight_3(3)
    weight_ready(3)
    partial(0, block(3))
    partial(1, block(-3))
    for j in range(4):
        reduce_send(0, 2 + j, up_order[j], None if j < 2 else j - 2)
        reduce_send(1, 2 + j, down_order[j], None if j < 2 else j - 2)
    for k in (2, 1):
        weight_2(k)
        if k == 2:
            weight_1(1)
        weight_3(k)
        weight_ready(k)
        partial(0, block(k))
        partial(1, block(-k))
        for j in range(4):
            idx = 4 * (3 - k) + 2 + j
            reduce_send(0, idx, up_order[j], idx - 4)
            reduce_send(1, idx, down_order[j], idx - 4)
    partial(0, z)

    def gather_copy(u, idx, b, r):
        return remote(
            res.at[b, r], res.at[b, r], z_send.at[2 + u], ag_recv.at[u, idx], head=up if u == 0 else down
        )

    loads[4].wait()
    for j, r in enumerate(gather_order):
        i_up = 10 + (2, 0, 3, 1)[j]
        i_down = 10 + (0, 2, 1, 3)[j]
        reduce_copy(0, i_up).wait_recv()
        reduce_copy(1, i_down).wait_recv()
        value = (pb[0, r] + ru[i_up].astype(F32) + rd[i_down].astype(F32)).astype(BF16)
        cols = pl.ds(pl.multiple_of(r * 128, 128), 128)
        ov[:, cols] = value
        res[z, r] = (value.astype(F32) - tb[:, cols].astype(F32)).astype(BF16)
        gather_copy(0, j, z, r).start()
        gather_copy(1, j, z, r).start()
    out_copy = pltpu.make_async_copy(ov, out_o, out_sem.at[0])
    out_copy.start()

    def residual_block(b, pieces):
        return jnp.concatenate([res[b, r] for r in pieces], axis=1)

    def grads(b, begin=False):
        term = dot(residual_block(b, range(4)), weight_block(b), NN)
        da[...] = term if begin else da[...] + term

    def weight_grads(b):
        row, cols = block_cols(b)
        d_b = dot(residual_block(b, range(4)), att[...], TN).astype(BF16)
        dw[row, cols] = d_b.reshape(2, 2, 128, ROWS)

    def dw_to_core(row, cols, level, slot):
        return remote(
            dw.at[row, cols, sibling], cw.at[level - 1, cols], d_send.at[0], dc_recv.at[slot], seq_2=sibling
        )

    every = pl.ds(0, 4)

    def dw_side(level, toward_right, whole):
        to = right if toward_right else left
        side = 0 if toward_right else 1
        sem = dx_recv.at[4 * (level - 1) + side + (0 if whole else 2)]
        if whole:
            return remote(xs.at[level - 1, to], xr.at[level - 1, side], d_send.at[1], sem, seq_1=to)
        part = first_half if toward_right else second_half
        return remote(
            xs.at[level - 1, across, part], xh.at[level - 1, side], d_send.at[1], sem, seq_1=to
        )

    def dw_1(level):
        row = level_row(level)
        if level < 4:
            dw_to_core(row, every, level, level - 1).wait_recv()
        else:
            dw_to_core(row, other_cols, level, 3).wait_recv()
            dw_to_core(row, pl.ds(first_col, 1), level, 4).wait_recv()
            dw_to_core(row, pl.ds(first_col + 1, 1), level, 5).wait_recv()
        for i, to in enumerate((across, right, left, x)):
            xs[level - 1, to] = (
                dw[row, to, c].astype(F32) + cw[level - 1, to].astype(F32)
            ).astype(BF16)
            if i == 0:
                dw_side(level, True, False).start()
                dw_side(level, False, False).start()

    def dw_2(level):
        for side, toward_right in enumerate((True, False)):
            to = right if toward_right else left
            part = first_half if toward_right else second_half
            dw_side(level, toward_right, False).wait_recv()
            value = xs[level - 1, to, part].astype(F32) + xh[level - 1, side].astype(F32)
            xs[level - 1, to, part] = value.astype(BF16)
            dw_side(level, toward_right, True).start()

    def dw_3(level):
        row = level_row(level)
        total = xs[level - 1, x].astype(F32)
        for side, toward_right in enumerate((True, False)):
            dw_side(level, toward_right, True).wait_recv()
            total = total + xr[level - 1, side].astype(F32)

        @pl.when(row == y)
        def _():
            yown[...] = total

        @pl.when(row != y)
        def _():
            ysend[level - 1] = total.astype(BF16)
            d = lax.rem(row - y + 4, 4)
            remote(
                ysend.at[level - 1], yrecv.at[d - 1], d_send.at[2], dy_recv.at[d - 1], seq_0=row
            ).start()

    first_col = 2 * lax.rem(block(4), 2)
    other_cols = pl.ds(2 - first_col, 2)

    grads(z, begin=True)
    weight_grads(z)
    for k in (1, 2, 3):
        for j, r in enumerate(gather_order):
            for u in (0, 1):
                b = block(-k if u == 0 else k)
                gather_copy(u, 4 * (k - 1) + j, b, r).wait_recv()
                if k < 3:
                    gather_copy(u, 4 * k + j, b, r).start()
                elif u == 0 and j < 2:
                    gather_copy(u, 12 + j, b, r).start()
                elif u == 1 and j >= 2:
                    gather_copy(u, 12 + j - 2, b, r).start()
            if k >= 2 and j == 0:
                dw_1(k - 1)
            if k >= 2 and j == 2:
                dw_2(k - 1)
            if k >= 3 and j == 1:
                dw_3(k - 2)

        @pl.loop(0, 2)
        def _(u, k=k):
            b = block(k * (2 * u - 1))
            grads(b)
            weight_grads(b)

        dw_to_core(level_row(k), every, k, k - 1).start()

    dw_to_core(level_row(4), other_cols, 4, 3).start()
    dw_3(2)
    dw_1(3)

    b4 = block(4)

    def last_half(i):
        col = first_col + i
        gather_copy(0, 12 + i, b4, gather_order[i]).wait_recv()
        gather_copy(1, 12 + i, b4, gather_order[2 + i]).wait_recv()
        term = dot(residual_block(b4, (2 * i, 2 * i + 1)), wf[row4, col].reshape(256, ROWS), NN)
        if i == 0:
            da[...] += term
        else:
            dab[...] = (da[...] + term).astype(BF16)

    def last_weight_half(i):
        col = first_col + i
        d_b = dot(residual_block(b4, (2 * i, 2 * i + 1)), att[...], TN).astype(BF16)
        dw[row4, col] = d_b.reshape(2, 128, ROWS)
        dw_to_core(row4, pl.ds(col, 1), 4, 4 + i).start()

    last_half(0)
    last_weight_half(0)
    dw_2(3)
    last_half(1)

    @pl.loop(0, HEADS)
    def _(h):
        cols = head_columns(h)
        tot[1, h] = dot(scaled[:, cols], dab[:, cols], TN)

    scan_begin(1)
    last_weight_half(1)
    scan_x(1)
    dw_1(4)
    dw_3(3)

    def gradient_pair(start):
        @pl.loop(start, start + 2)
        def _(h):
            cols = head_columns(h)
            mixed = jnp.where(causal, dot(dab[:, cols], vb[:, cols], NT), 0.0).astype(BF16)
            g = dot(dab[:, cols], state[0, h], NT) + dot(mixed, kb[:, cols], NN)
            oq[:, cols] = (g * scale).astype(BF16)
            gk_acc[:, cols] = dot(mixed, scaled[:, cols], TN)
            gv_acc[:, cols] = dot(scores[h], dab[:, cols], TN)

    gradient_pair(0)
    dw_2(4)
    gradient_pair(2)
    scan_y(1, True)
    q_copy = pltpu.make_async_copy(oq, gq_o, out_sem.at[1])
    q_copy.start()
    dw_3(4)
    scan_core(1, True)
    scan_end(1, True)
    out_copy.wait()

    @pl.loop(0, HEADS)
    def _(h):
        cols = head_columns(h)
        ok[:, cols] = (gk_acc[:, cols] + dot(vb[:, cols], state[1, h], NT)).astype(BF16)
        ov[:, cols] = (gv_acc[:, cols] + dot(kb[:, cols], state[1, h], NN)).astype(BF16)

    k_copy = pltpu.make_async_copy(ok, gk_o, out_sem.at[2])
    k_copy.start()
    v_copy = pltpu.make_async_copy(ov, gv_o, out_sem.at[3])
    v_copy.start()
    total = yown[...]
    for d in (1, 3, 2):
        remote(
            yrecv.at[d - 1], yrecv.at[d - 1], d_send.at[2], dy_recv.at[d - 1], seq_0=lax.rem(y + d, 4)
        ).wait_recv()
        total = total + yrecv[d - 1].astype(F32)
    yown[...] = total * weight_factor
    w_copy = pltpu.make_async_copy(yown, gw_o, out_sem.at[4])
    w_copy.start()

    wait_bytes(su, z_send.at[0])
    wait_bytes(sd, z_send.at[1])
    wait_bytes(su, z_send.at[2])
    wait_bytes(sd, z_send.at[3])
    wait_bytes(yrecv, w_send.at[0])
    wait_bytes(su.at[pl.ds(0, 12)], w_send.at[1])
    wait_bytes(xs, w_send.at[2])
    wait_bytes(cw, d_send.at[0])
    wait_bytes(su.at[pl.ds(0, 12)], d_send.at[1])
    wait_bytes(yrecv, d_send.at[2])
    for n in (0, 1):
        wait_bytes(loc.at[n], sc_send.at[n, 0])
        wait_bytes(xrc.at[n], sc_send.at[n, 1])
        wait_bytes(yrc.at[n], sc_send.at[n, 2])
        wait_bytes(pfs.at[n], sc_send.at[n, 3])
    for copy in (q_copy, k_copy, v_copy, w_copy):
        copy.wait()


def write_out(*refs):
    sems = refs[-1]
    copies = [pltpu.make_async_copy(refs[i], refs[5 + i], sems.at[i]) for i in range(5)]
    for copy in copies:
        copy.start()
    for copy in copies:
        copy.wait()


def on_device(query_rows, key_rows, value_rows, out_weight, target_rows):
    rows = jax.ShapeDtypeStruct((ROWS, ROWS), BF16)
    total_rows = query_rows.shape[0] * lax.axis_size(SEQ)
    full = (ROWS, ROWS)
    vm = pltpu.VMEM
    scratch = (
        [vm(full, BF16)] * 5
        + [
            vm((4, 4, 2, 128, ROWS), BF16),
            vm(full, BF16),
            vm((2, 4, ROWS, 128), F32),
        ]
        + [vm((14, ROWS, 128), BF16)] * 4
        + [
            vm((8, 4, ROWS, 128), BF16),
            vm(full, F32),
            vm(full, BF16),
            vm((4, 4, 2, 128, ROWS), BF16),
            vm((4, 4, 128, ROWS), BF16),
            vm((4, 4, 128, ROWS), BF16),
            vm((4, 2, 64, ROWS), BF16),
            vm((4, 2, 128, ROWS), BF16),
            vm((4, 128, ROWS), BF16),
            vm((128, ROWS), F32),
            vm((3, 128, ROWS), BF16),
            vm((HEADS, ROWS, ROWS), BF16),
            vm(full, F32),
            vm(full, F32),
        ]
        + [vm(full, BF16)] * 3
        + [
            vm((2, HEADS, DH, DH), F32),
            vm((2, HEADS, DH, DH), BF16),
            vm((2, HEADS, DH, DH), BF16),
            vm((2, 2, DH, DH), BF16),
            vm((2, 3, 2, DH, DH), BF16),
            vm((2, 2, DH, DH), BF16),
            vm((2, 3, 2, DH, DH), BF16),
            vm((2, 2, DH, DH), BF16),
            vm((2, 2, DH, DH), BF16),
            vm((2, 2, DH, DH), F32),
            vm((2, HEADS, DH, DH), BF16),
        ]
    )
    dma = pltpu.SemaphoreType.DMA
    scratch += [
        dma((5,)), dma((5,)), dma((2, 14)), dma((2, 14)), dma((4,)), dma((3,)), dma((16,)), dma((16,)),
        dma((3,)), dma((2, 8)), dma((2, 4)), dma((6,)), dma((16,)), dma((3,)), dma((3,)),
    ]
    anywhere = pl.BlockSpec(memory_space=pl.ANY)

    arguments = (query_rows, key_rows, value_rows, out_weight, target_rows)

    def body(*refs):
        kernel(1.0 / math.sqrt(total_rows), *refs)

    shapes = (rows, rows, rows, rows, jax.ShapeDtypeStruct((128, ROWS), F32))
    results = pl.pallas_call(
        body,
        out_shape=shapes,
        in_specs=[pl.BlockSpec(memory_space=pltpu.HBM)] * 5,
        out_specs=(anywhere,) * 5,
        scratch_shapes=scratch,
        compiler_params=pltpu.CompilerParams(
            collective_id=0, has_side_effects=True, vmem_limit_bytes=48 * 1024 * 1024
        ),
        name="linear_attention",
    )(*(pltpu.with_memory_space_constraint(a, pltpu.HBM) for a in arguments))
    return pl.pallas_call(
        write_out,
        out_shape=shapes,
        in_specs=[anywhere] * 5,
        out_specs=(pl.BlockSpec(memory_space=pltpu.HBM),) * 5,
        scratch_shapes=[dma((5,))],
        compiler_params=pltpu.CompilerParams(vmem_limit_bytes=1024 * 1024),
        name="write_out",
    )(*results)


def solution(mesh):
    torus = Mesh(
        mesh.devices.reshape(4, 4, 2, mesh.shape["head"]), ("seq_0", "seq_1", "seq_2", "head")
    )
    spec = P(SEQ, "head")
    return jax.shard_map(
        on_device, mesh=torus, in_specs=(spec,) * 5, out_specs=(spec,) * 5, check_vma=False
    )
```

time: 142 us -> 132 us (0.930)
  local copies, waits for them, and re-layouts: 6.18 us -> 0 us
  Pallas kernels: 135 us -> 131 us
    unnamed x13 -> x0, local copies, waits for them, and re-layouts: 6.18 us -> none
    pallas_call x1 -> x2, Pallas kernels: 135 us -> 131 us  [the longest x1 130 us: on_device(): pl.pallas_call(body, out_shape=shapes, in_specs=[pl.BlockSpec(memory_spac...]
where the time goes in v2:
time: 132 us
  Pallas kernels  131 us (99%)
    pallas_call x1, Pallas kernels, on_device(): pl.pallas_call(body, out_shape=shapes, in_specs=[pl.BlockSpec(memory_spac...  130 us

profile of v2, /device:TPU:16, one launch (start us, length us, event | category | flops | bytes accessed | tf_op | source)
XLA Modules:
  0.0 131.9 jit_solution(1465498131578784321)
XLA Ops:
  0.6 129.8 %linear_attention.1 = (bf16[512,512]{1,0:T(8,128)(2,1)S(1)}, bf16[512,512]{1,0:T(8,128)(2,1)S(1)}, bf16[512,512]{1,0:T(8,128)(2,1)S(1)}, bf16[512,512]{1,0:T(8,128)(2,1)S(1)}, f32[128,512]{1,0:T(8,128)S(1)}) custom-call(bf16[512,512]{1,0:T(8,128)(2,1)} %refs_0_.1, bf16[512,512]{1,0:T(8,128)(2,1)} %refs_1_.1, bf16[512,512]{1,0:T(8,128)(2,1)} %refs_2_.1, ...), custom_call_target="tpu_custom_call" | custom-call | tf_op jit(solution)/shard_map/linear_attention/pallas_call | solution.py:618
  130.5 1.4 %write_out.1 = (bf16[512,512]{1,0:T(8,128)(2,1)}, bf16[512,512]{1,0:T(8,128)(2,1)}, bf16[512,512]{1,0:T(8,128)(2,1)}, bf16[512,512]{1,0:T(8,128)(2,1)}, f32[128,512]{1,0:T(8,128)}) custom-call(bf16[512,512]{1,0:T(8,128)(2,1)S(1)} %get-tuple-element.10.refs_0_, bf16[512,512]{1,0:T(8,128)(2,1)S(1)} %get-tuple-element.11.refs_1_, ...), custom_call_target="tpu_custom_call" | custom-call | tf_op jit(solution)/shard_map/write_out/pallas_call | solution.py:629

commit v3 on v2

--- a/solution.py
+++ b/solution.py
@@ -40,9 +40,9 @@
     out_o, gq_o, gk_o, gv_o, gw_o,
     qb, kb, vb, tb, scaled, wf, att, pb, su, sd, ru, rd, res, da, dab, dw, cw, xs, xh, xr, ysend, yown, yrecv,
     scores, gk_acc, gv_acc, oq, ok, ov,
-    tot, loc, sib, ct, xrc, rt, yrc, pfs, pfr, px, state,
+    tot, loc, sib, ct, xrc, rt, yrc, pfs, pfr, px, state, h1, h2, h2r, hk, h3, h3r,
     in_sem, out_sem, rs_recv, ag_recv, z_send, wy_recv, wx_recv, wc_recv, w_send, sc_recv, sc_send,
-    dc_recv, dx_recv, dy_recv, d_send,
+    dc_recv, dx_recv, dy_recv, d_send, q1_recv, q2_recv, q2_send, q3_recv, q3_send,
 ):
     y = lax.axis_index("seq_0")
     x = lax.axis_index("seq_1")
@@ -84,27 +84,36 @@
         pl.semaphore_signal(barrier, inc=1, device_id=partner, device_id_type=MESH)
     pl.semaphore_wait(barrier, len(partners))
 
-    def weight_y():
+    def weight_parts(level):
+        return (first_half, second_half) if level >= 3 else (pl.ds(0, 128),)
+
+    def weight_y_copy(level, row, part, d):
+        ref = wf.at[row, x, c, weight_parts(level)[part]]
+        return remote(ref, ref, w_send.at[0], wy_recv.at[3 * part + d - 1], seq_0=lax.rem(row + d, 4))
+
+    def weight_y(level):
         for d in (2, 3, 1):
-            remote(
-                wf.at[y, x, c], wf.at[y, x, c], w_send.at[0], wy_recv.at[d - 1], seq_0=lax.rem(y + d, 4)
-            ).start()
+            for part in range(len(weight_parts(level))):
+                weight_y_copy(level, y, part, d).start()
 
     def weight_to_core(row, col, slot):
         return remote(
             wf.at[row, col, c], wf.at[row, col, c], w_send.at[2], wc_recv.at[slot], seq_2=sibling
         )
 
-    def weight_side(level, toward_right, whole):
+    def weight_side(level, toward_right, part):
         row = level_row(level)
         to, source = (right, left) if toward_right else (left, right)
-        slot = 4 * (level - 1) + (0 if toward_right else 1) + (0 if whole else 2)
-        sem = wx_recv.at[slot]
-        if whole:
-            sent, got = wf.at[row, x, c], wf.at[row, source, c]
+        side = 0 if toward_right else 1
+        if part is None:
+            rows = first_half if toward_right else second_half
+            sent, got = wf.at[row, source, c, rows], wf.at[row, across, c, rows]
+            slot = 4 + side
         else:
-            part = first_half if toward_right else second_half
-            sent, got = wf.at[row, source, c, part], wf.at[row, across, c, part]
+            rows = weight_parts(level)[part]
+            sent, got = wf.at[row, x, c, rows], wf.at[row, source, c, rows]
+            slot = 2 * side + part
+        sem = wx_recv.at[6 * (level - 1) + slot]
         return (
             lambda: remote(sent, sent, w_send.at[1], sem, seq_1=to).start(),
             lambda: remote(got, got, w_send.at[1], sem, seq_1=to).wait_recv(),
@@ -112,29 +121,34 @@
 
     def weight_1(level):
         row = level_row(level)
-
-        @pl.when(row != y)
-        def _():
-            d = lax.rem(y - row + 4, 4)
-            remote(
-                wf.at[row, x, c], wf.at[row, x, c], w_send.at[0], wy_recv.at[d - 1], seq_0=row
-            ).wait_recv()
-
-        weight_side(level, True, True)[0]()
-        weight_side(level, False, True)[0]()
+        for part in range(len(weight_parts(level))):
+
+            @pl.when(row != y)
+            def _():
+                weight_y_copy(level, row, part, lax.rem(y - row + 4, 4)).wait_recv()
+
+            weight_side(level, True, part)[0]()
+            weight_side(level, False, part)[0]()
         weight_to_core(row, x, 4 * (level - 1)).start()
 
     def weight_2(level):
         row = level_row(level)
-        for i, toward_right in enumerate((True, False)):
-            weight_side(level, toward_right, True)[1]()
-            weight_side(level, toward_right, False)[0]()
-            weight_to_core(row, left if toward_right else right, 4 * (level - 1) + 1 + i).start()
+        last = len(weight_parts(level)) - 1
+        weight_side(level, True, 0)[1]()
+        weight_side(level, True, None)[0]()
+        if last:
+            weight_side(level, False, 0)[1]()
+        weight_side(level, False, last)[1]()
+        weight_side(level, False, None)[0]()
+        if last:
+            weight_side(level, True, 1)[1]()
+        weight_to_core(row, left, 4 * (level - 1) + 1).start()
+        weight_to_core(row, right, 4 * (level - 1) + 2).start()
 
     def weight_3(level):
         row = level_row(level)
         for toward_right in (True, False):
-            weight_side(level, toward_right, False)[1]()
+            weight_side(level, toward_right, None)[1]()
         weight_to_core(row, across, 4 * (level - 1) + 3).start()
 
     def weight_ready(level):
@@ -150,7 +164,7 @@
 
     @pl.when(level_row(4) == y)
     def _():
-        weight_y()
+        weight_y(4)
 
     def head_columns(h):
         return pl.ds(pl.multiple_of(h * DH, DH), DH)
@@ -159,54 +173,65 @@
         loc[n] = tot[n].astype(BF16)
         remote(loc.at[n], sib.at[n], sc_send.at[n, 0], sc_recv.at[n, 0], seq_2=sibling).start()
 
-    mine = pl.ds(2 * c, 2)
+    def scan_x_copy(n, i, d):
+        return remote(
+            ct.at[n, i], xrc.at[n, d - 1, i], sc_send.at[n, 1], sc_recv.at[n, 3 * i + d],
+            seq_1=lax.rem(x + d, 4),
+        )
+
+    def scan_y_copy(n, i, d):
+        return remote(
+            rt.at[n, i], yrc.at[n, d - 1, i], sc_send.at[n, 2], sc_recv.at[n, 6 + 3 * i + d],
+            seq_0=lax.rem(y + d, 4),
+        )
+
+    def scan_core_copy(n, i):
+        return remote(
+            pfs.at[n, i], pfr.at[n, i], sc_send.at[n, 3], sc_recv.at[n, 13 + i], seq_2=sibling
+        )
 
     def scan_x(n):
         remote(sib.at[n], sib.at[n], sc_send.at[n, 0], sc_recv.at[n, 0], seq_2=sibling).wait_recv()
-        chip = tot[n, mine] + sib[n, mine].astype(F32)
-        ct[n] = chip.astype(BF16)
-        for d in (2, 1, 3):
-            remote(
-                ct.at[n], xrc.at[n, d - 1], sc_send.at[n, 1], sc_recv.at[n, d], seq_1=lax.rem(x + d, 4)
-            ).start()
+        for i in (0, 1):
+            chip = tot[n, 2 * c + i] + sib[n, 2 * c + i].astype(F32)
+            ct[n, i] = chip.astype(BF16)
+            for d in (2, 1, 3):
+                scan_x_copy(n, i, d).start()
 
     def scan_y(n, reverse):
-        total = ct[n].astype(F32)
-        passed = jnp.zeros((2, DH, DH), F32)
-        for d in (1, 3, 2):
-            remote(
-                ct.at[n], xrc.at[n, d - 1], sc_send.at[n, 1], sc_recv.at[n, d], seq_1=lax.rem(x + d, 4)
-            ).wait_recv()
-            piece = xrc[n, d - 1].astype(F32)
-            total = total + piece
-            counts = (d > x) if reverse else (d <= x)
-            passed = passed + piece * counts.astype(F32)
-        rt[n] = total.astype(BF16)
-        px[n] = passed
-        for d in (2, 1, 3):
-            remote(
-                rt.at[n], yrc.at[n, d - 1], sc_send.at[n, 2], sc_recv.at[n, 3 + d], seq_0=lax.rem(y + d, 4)
-            ).start()
+        for i in (0, 1):
+            total = ct[n, i].astype(F32)
+            passed = jnp.zeros((DH, DH), F32)
+            for d in (1, 3, 2):
+                scan_x_copy(n, i, d).wait_recv()
+                piece = xrc[n, d - 1, i].astype(F32)
+                total = total + piece
+                counts = (d > x) if reverse else (d <= x)
+                passed = passed + piece * counts.astype(F32)
+            rt[n, i] = total.astype(BF16)
+            px[n, i] = passed
+            for d in (2, 1, 3):
+                scan_y_copy(n, i, d).start()
 
     def scan_core(n, reverse):
-        passed = px[n]
-        for d in (1, 3, 2):
-            remote(
-                rt.at[n], yrc.at[n, d - 1], sc_send.at[n, 2], sc_recv.at[n, 3 + d], seq_0=lax.rem(y + d, 4)
-            ).wait_recv()
-            counts = (d > y) if reverse else (d <= y)
-            passed = passed + yrc[n, d - 1].astype(F32) * counts.astype(F32)
-        px[n] = passed
-        pfs[n] = passed.astype(BF16)
-        remote(pfs.at[n], pfr.at[n], sc_send.at[n, 3], sc_recv.at[n, 7], seq_2=sibling).start()
+        for i in (0, 1):
+            passed = px[n, i]
+            for d in (1, 3, 2):
+                scan_y_copy(n, i, d).wait_recv()
+                counts = (d > y) if reverse else (d <= y)
+                passed = passed + yrc[n, d - 1, i].astype(F32) * counts.astype(F32)
+            px[n, i] = passed
+            pfs[n, i] = passed.astype(BF16)
+            scan_core_copy(n, i).start()
 
     def scan_end(n, reverse):
-        remote(pfs.at[n], pfr.at[n], sc_send.at[n, 3], sc_recv.at[n, 7], seq_2=sibling).wait_recv()
         own_core = (c == 0) if reverse else (c == 1)
         factor = own_core.astype(F32)
-        theirs = pl.ds(2 * sibling, 2)
-        state[n, mine] = (px[n] + sib[n, mine].astype(F32) * factor).astype(BF16)
-        state[n, theirs] = (pfr[n].astype(F32) + sib[n, theirs].astype(F32) * factor).astype(BF16)
+        for i in (0, 1):
+            ours, theirs = 2 * c + i, 2 * sibling + i
+            state[n, ours] = (px[n, i] + sib[n, ours].astype(F32) * factor).astype(BF16)
+            scan_core_copy(n, i).wait_recv()
+            state[n, theirs] = (pfr[n, i].astype(F32) + sib[n, theirs].astype(F32) * factor).astype(BF16)
 
     loads[1].wait()
     loads[2].wait()
@@ -220,7 +245,7 @@
 
     @pl.when(level_row(3) == y)
     def _():
-        weight_y()
+        weight_y(3)
 
     first = lax.rem((y * 4 + x) * 2 + c, 32) * ROWS
     positions = (first + lax.broadcasted_iota(jnp.int32, (ROWS, 1), 0) + 1).astype(F32)
@@ -250,10 +275,10 @@
 
     @pl.when(jnp.logical_and(level_row(4) != y, level_row(3) != y))
     def _():
-        weight_y()
-
+        weight_y(1)
+
+    weight_1(3)
     weight_2(4)
-    weight_1(3)
     scan_core(0, False)
     weight_3(4)
     scan_end(0, False)
@@ -265,7 +290,7 @@
 
     up_order = (2 + c, 3 - c, c, 1 - c)
     down_order = (c, 1 - c, 2 + c, 3 - c)
-    gather_order = (c, 2 + c, 1 - c, 3 - c)
+    gather_order = (c, 1 - c, 2 + c, 3 - c)
 
     def block_cols(b):
         return lax.div(b, 2), pl.ds(2 * lax.rem(b, 2), 2)
@@ -333,8 +358,8 @@
 
     loads[4].wait()
     for j, r in enumerate(gather_order):
-        i_up = 10 + (2, 0, 3, 1)[j]
-        i_down = 10 + (0, 2, 1, 3)[j]
+        i_up = 10 + (2, 3, 0, 1)[j]
+        i_down = 10 + j
         reduce_copy(0, i_up).wait_recv()
         reduce_copy(1, i_down).wait_recv()
         value = (pb[0, r] + ru[i_up].astype(F32) + rd[i_down].astype(F32)).astype(BF16)
@@ -378,12 +403,7 @@
 
     def dw_1(level):
         row = level_row(level)
-        if level < 4:
-            dw_to_core(row, every, level, level - 1).wait_recv()
-        else:
-            dw_to_core(row, other_cols, level, 3).wait_recv()
-            dw_to_core(row, pl.ds(first_col, 1), level, 4).wait_recv()
-            dw_to_core(row, pl.ds(first_col + 1, 1), level, 5).wait_recv()
+        dw_to_core(row, every, level, level - 1).wait_recv()
         for i, to in enumerate((across, right, left, x)):
             xs[level - 1, to] = (
                 dw[row, to, c].astype(F32) + cw[level - 1, to].astype(F32)
@@ -421,27 +441,134 @@
             ).start()
 
     first_col = 2 * lax.rem(block(4), 2)
-    other_cols = pl.ds(2 - first_col, 2)
+    other_col = 2 - first_col
+    row3 = level_row(3)
+    piece_cols = (
+        first_col, first_col + 1, other_col, other_col, other_col + 1, other_col + 1, first_col, first_col + 1
+    )
+    piece_rows = (row3, row3, row3, row4, row3, row4, row4, row4)
+    piece_group = (2, 2, 2, 3, 2, 3, 3, 3)
+
+    def lanes(q):
+        return pl.ds(pl.multiple_of(q * 128, 128), 128)
+
+    def along(x_axis, to):
+        return {"seq_1": to} if x_axis else {"seq_0": to}
+
+    def piece_to_core(p, count=1):
+        cols = pl.ds(piece_cols[p], count)
+        return remote(
+            dw.at[piece_rows[p], cols, sibling], cw.at[piece_group[p], cols], d_send.at[0],
+            dc_recv.at[2 + p], seq_2=sibling,
+        )
+
+    def quarter_copy(p, d):
+        x_axis = p < 6
+        to = lax.rem((x if x_axis else y) + d, 4)
+        return remote(
+            xs.at[piece_group[p], piece_cols[p], :, lanes(to)], h1.at[p, d - 1], d_send.at[3],
+            q1_recv.at[p, d - 1], **along(x_axis, to),
+        )
+
+    def quarter_place(p):
+        to_col = lax.rem(piece_cols[p] - x + 4, 4)
+        to_row = lax.rem(piece_rows[p] - y + 4, 4)
+        return (to_row, to_col) if p < 6 else (to_col, to_row)
+
+    def quarter_1(p):
+        row, col, group = piece_rows[p], piece_cols[p], piece_group[p]
+        if p == 0:
+            piece_to_core(0, 2).wait_recv()
+        elif p != 1:
+            piece_to_core(p).wait_recv()
+        xs[group, col] = (dw[row, col, c].astype(F32) + cw[group, col].astype(F32)).astype(BF16)
+        for d in (2, 1, 3):
+            quarter_copy(p, d).start()
+
+    def quarter_2(p):
+        total = xs[piece_group[p], piece_cols[p], :, lanes(x if p < 6 else y)].astype(F32)
+        for d in (1, 3, 2):
+            quarter_copy(p, d).wait_recv()
+            total = total + h1[p, d - 1].astype(F32)
+        away, _ = quarter_place(p)
+        hk[p] = total
+
+        @pl.when(away != 0)
+        def _():
+            h2[p] = total.astype(BF16)
+            to = piece_rows[p] if p < 6 else piece_cols[p]
+            remote(
+                h2.at[p], h2r.at[p, away - 1], q2_send.at[p], q2_recv.at[p, away - 1], **along(p >= 6, to)
+            ).start()
+
+    def quarter_3(p):
+        away, rest = quarter_place(p)
+
+        @pl.when(away == 0)
+        def _():
+            total = hk[p]
+            for d in (1, 3, 2):
+                remote(
+                    h2r.at[p, d - 1], h2r.at[p, d - 1], q2_send.at[p], q2_recv.at[p, d - 1],
+                    **along(p >= 6, lax.rem((x if p >= 6 else y) + d, 4)),
+                ).wait_recv()
+                total = total + h2r[p, d - 1].astype(F32)
+
+            @pl.when(rest == 0)
+            def _():
+                yown[:, lanes(x if p < 6 else y)] = total
+
+            @pl.when(rest != 0)
+            def _():
+                h3[p] = total.astype(BF16)
+                group = 0 if p < 6 else 1
+                to = piece_cols[p] if p < 6 else piece_rows[p]
+                remote(
+                    h3.at[p], h3r.at[group, rest - 1], q3_send.at[p], q3_recv.at[group, rest - 1],
+                    **along(p < 6, to),
+                ).start()
+
+    def quarter_end(group):
+        axis_place = x if group == 0 else y
+        for d in (1, 3, 2):
+            remote(
+                h3r.at[group, d - 1], h3r.at[group, d - 1], q3_send.at[0], q3_recv.at[group, d - 1],
+                **along(group == 0, lax.rem(axis_place + d, 4)),
+            ).wait_recv()
+            yown[:, lanes(lax.rem(axis_place - d + 4, 4))] = h3r[group, d - 1].astype(F32)
 
     grads(z, begin=True)
     weight_grads(z)
-    for k in (1, 2, 3):
-        for j, r in enumerate(gather_order):
-            for u in (0, 1):
-                b = block(-k if u == 0 else k)
-                gather_copy(u, 4 * (k - 1) + j, b, r).wait_recv()
-                if k < 3:
-                    gather_copy(u, 4 * k + j, b, r).start()
-                elif u == 0 and j < 2:
-                    gather_copy(u, 12 + j, b, r).start()
-                elif u == 1 and j >= 2:
-                    gather_copy(u, 12 + j - 2, b, r).start()
-            if k >= 2 and j == 0:
-                dw_1(k - 1)
-            if k >= 2 and j == 2:
-                dw_2(k - 1)
-            if k >= 3 and j == 1:
-                dw_3(k - 2)
+    def half_block(b, i):
+        row, cols = block_cols(b)
+        col = 2 * lax.rem(b, 2) + i
+        pieces = residual_block(b, (2 * i, 2 * i + 1))
+        d_b = dot(pieces, att[...], TN).astype(BF16)
+        dw[row, col] = d_b.reshape(2, 128, ROWS)
+        return dot(pieces, wf[row, col].reshape(256, ROWS), NN)
+
+    def both_halves(i):
+        @pl.loop(0, 2)
+        def _(u):
+            da[...] += half_block(block(3 * (2 * u - 1)), i)
+
+    def chunk(k, j):
+        r = gather_order[j]
+        for u in (0, 1):
+            b = block(-k if u == 0 else k)
+            gather_copy(u, 4 * (k - 1) + j, b, r).wait_recv()
+            if k < 3:
+                gather_copy(u, 4 * k + j, b, r).start()
+            elif j % 2 == u:
+                gather_copy(u, 12 + j // 2, b, r).start()
+
+    for k in (1, 2):
+        for j in range(4):
+            chunk(k, j)
+            if k == 2 and j == 0:
+                dw_1(1)
+            if k == 2 and j == 2:
+                dw_2(1)
 
         @pl.loop(0, 2)
         def _(u, k=k):
@@ -450,32 +577,50 @@
             weight_grads(b)
 
         dw_to_core(level_row(k), every, k, k - 1).start()
-
-    dw_to_core(level_row(4), other_cols, 4, 3).start()
+    piece_to_core(0, 2).start()
+    chunk(3, 0)
+    dw_1(2)
+    quarter_1(0)
+    quarter_1(1)
+    chunk(3, 1)
+    both_halves(0)
+    piece_to_core(2).start()
+    piece_to_core(3).start()
+    dw_3(1)
+    chunk(3, 2)
+    dw_2(2)
+    quarter_1(2)
+    quarter_1(3)
+    quarter_2(0)
+    quarter_2(1)
+    chunk(3, 3)
+    both_halves(1)
+    piece_to_core(4).start()
+    piece_to_core(5).start()
     dw_3(2)
-    dw_1(3)
 
     b4 = block(4)
 
     def last_half(i):
-        col = first_col + i
-        gather_copy(0, 12 + i, b4, gather_order[i]).wait_recv()
-        gather_copy(1, 12 + i, b4, gather_order[2 + i]).wait_recv()
-        term = dot(residual_block(b4, (2 * i, 2 * i + 1)), wf[row4, col].reshape(256, ROWS), NN)
+        gather_copy(0, 12 + i, b4, gather_order[2 * i]).wait_recv()
+        gather_copy(1, 12 + i, b4, gather_order[2 * i + 1]).wait_recv()
+        term = dot(residual_block(b4, (2 * i, 2 * i + 1)), wf[row4, first_col + i].reshape(256, ROWS), NN)
         if i == 0:
             da[...] += term
         else:
             dab[...] = (da[...] + term).astype(BF16)
 
     def last_weight_half(i):
-        col = first_col + i
         d_b = dot(residual_block(b4, (2 * i, 2 * i + 1)), att[...], TN).astype(BF16)
-        dw[row4, col] = d_b.reshape(2, 128, ROWS)
-        dw_to_core(row4, pl.ds(col, 1), 4, 4 + i).start()
+        dw[row4, first_col + i] = d_b.reshape(2, 128, ROWS)
+        piece_to_core(6 + i).start()
 
     last_half(0)
     last_weight_half(0)
-    dw_2(3)
+    quarter_2(2)
+    quarter_2(3)
+    quarter_1(4)
+    quarter_1(5)
     last_half(1)
 
     @pl.loop(0, HEADS)
@@ -486,8 +631,10 @@
     scan_begin(1)
     last_weight_half(1)
     scan_x(1)
-    dw_1(4)
-    dw_3(3)
+    quarter_1(6)
+    quarter_1(7)
+    quarter_3(0)
+    quarter_3(1)
 
     def gradient_pair(start):
         @pl.loop(start, start + 2)
@@ -500,12 +647,18 @@
             gv_acc[:, cols] = dot(scores[h], dab[:, cols], TN)
 
     gradient_pair(0)
-    dw_2(4)
+    quarter_2(4)
+    quarter_2(5)
+    quarter_3(2)
+    quarter_3(3)
     gradient_pair(2)
     scan_y(1, True)
     q_copy = pltpu.make_async_copy(oq, gq_o, out_sem.at[1])
     q_copy.start()
-    dw_3(4)
+    quarter_2(6)
+    quarter_2(7)
+    for p in range(4, 8):
+        quarter_3(p)
     scan_core(1, True)
     scan_end(1, True)
     out_copy.wait()
@@ -520,13 +673,30 @@
     k_copy.start()
     v_copy = pltpu.make_async_copy(ov, gv_o, out_sem.at[3])
     v_copy.start()
-    total = yown[...]
-    for d in (1, 3, 2):
-        remote(
-            yrecv.at[d - 1], yrecv.at[d - 1], d_send.at[2], dy_recv.at[d - 1], seq_0=lax.rem(y + d, 4)
-        ).wait_recv()
-        total = total + yrecv[d - 1].astype(F32)
-    yown[...] = total * weight_factor
+
+    in_last = jnp.logical_or(row3 == y, row4 == y)
+
+    @pl.when(jnp.logical_not(in_last))
+    def _():
+        total = yown[...]
+        for d in (1, 3, 2):
+            remote(
+                yrecv.at[d - 1], yrecv.at[d - 1], d_send.at[2], dy_recv.at[d - 1], seq_0=lax.rem(y + d, 4)
+            ).wait_recv()
+            total = total + yrecv[d - 1].astype(F32)
+        yown[...] = total
+
+    in_second = jnp.logical_and(row4 == y, lax.div(x, 2) == lax.div(first_col, 2))
+
+    @pl.when(jnp.logical_and(in_last, jnp.logical_not(in_second)))
+    def _():
+        quarter_end(0)
+
+    @pl.when(in_second)
+    def _():
+        quarter_end(1)
+
+    yown[...] = yown[...] * weight_factor
     w_copy = pltpu.make_async_copy(yown, gw_o, out_sem.at[4])
     w_copy.start()
 
@@ -538,8 +708,28 @@
     wait_bytes(su.at[pl.ds(0, 12)], w_send.at[1])
     wait_bytes(xs, w_send.at[2])
     wait_bytes(cw, d_send.at[0])
-    wait_bytes(su.at[pl.ds(0, 12)], d_send.at[1])
-    wait_bytes(yrecv, d_send.at[2])
+    wait_bytes(su.at[pl.ds(0, 6)], d_send.at[1])
+
+    @pl.when(in_last)
+    def _():
+        wait_bytes(yrecv.at[pl.ds(0, 2)], d_send.at[2])
+
+    @pl.when(jnp.logical_not(in_last))
+    def _():
+        wait_bytes(yrecv.at[0], d_send.at[2])
+
+    wait_bytes(su.at[pl.ds(0, 6)], d_send.at[3])
+    for p in range(8):
+        away, rest = quarter_place(p)
+
+        @pl.when(away != 0)
+        def _(p=p):
+            wait_bytes(h2.at[p], q2_send.at[p])
+
+        @pl.when(jnp.logical_and(away == 0, rest != 0))
+        def _(p=p):
+            wait_bytes(h3.at[p], q3_send.at[p])
+
     for n in (0, 1):
         wait_bytes(loc.at[n], sc_send.at[n, 0])
         wait_bytes(xrc.at[n], sc_send.at[n, 1])
@@ -600,12 +790,19 @@
             vm((2, 2, DH, DH), BF16),
             vm((2, 2, DH, DH), F32),
             vm((2, HEADS, DH, DH), BF16),
+            vm((8, 3, 128, 128), BF16),
+            vm((8, 128, 128), BF16),
+            vm((8, 3, 128, 128), BF16),
+            vm((8, 128, 128), F32),
+            vm((8, 128, 128), BF16),
+            vm((2, 3, 128, 128), BF16),
         ]
     )
     dma = pltpu.SemaphoreType.DMA
     scratch += [
-        dma((5,)), dma((5,)), dma((2, 14)), dma((2, 14)), dma((4,)), dma((3,)), dma((16,)), dma((16,)),
-        dma((3,)), dma((2, 8)), dma((2, 4)), dma((6,)), dma((16,)), dma((3,)), dma((3,)),
+        dma((5,)), dma((5,)), dma((2, 14)), dma((2, 14)), dma((4,)), dma((6,)), dma((24,)), dma((16,)),
+        dma((3,)), dma((2, 15)), dma((2, 4)), dma((10,)), dma((8,)), dma((3,)), dma((4,)),
+        dma((8, 3)), dma((8, 3)), dma((8,)), dma((2, 3)), dma((8,)),
     ]
     anywhere = pl.BlockSpec(memory_space=pl.ANY)
 

time: 132 us -> 127 us (0.962); the launches traced: 132 us -> 125 us
  Pallas kernels: 131 us -> 124 us
    pallas_call x1, Pallas kernels: 130 us -> 123 us  [on_device(): pl.pallas_call(body, out_shape=shapes, in_specs=[pl.BlockSpec(memory_spac...]
where the time goes in v3:
time: 127 us; the launch traced here: 125 us
  Pallas kernels  124 us (98%)
    pallas_call x1, Pallas kernels, on_device(): pl.pallas_call(body, out_shape=shapes, in_specs=[pl.BlockSpec(memory_spac...  123 us

profile of v3, /device:TPU:16, one launch (start us, length us, event | category | flops | bytes accessed | tf_op | source)
XLA Modules:
  0.0 125.1 jit_solution(11011050931031826088)
XLA Ops:
  0.6 123.0 %linear_attention.1 = (bf16[512,512]{1,0:T(8,128)(2,1)S(1)}, bf16[512,512]{1,0:T(8,128)(2,1)S(1)}, bf16[512,512]{1,0:T(8,128)(2,1)S(1)}, bf16[512,512]{1,0:T(8,128)(2,1)S(1)}, f32[128,512]{1,0:T(8,128)S(1)}) custom-call(bf16[512,512]{1,0:T(8,128)(2,1)} %refs_0_.1, bf16[512,512]{1,0:T(8,128)(2,1)} %refs_1_.1, bf16[512,512]{1,0:T(8,128)(2,1)} %refs_2_.1, ...), custom_call_target="tpu_custom_call" | custom-call | tf_op jit(solution)/shard_map/linear_attention/pallas_call | solution.py:815
  123.7 1.4 %write_out.1 = (bf16[512,512]{1,0:T(8,128)(2,1)}, bf16[512,512]{1,0:T(8,128)(2,1)}, bf16[512,512]{1,0:T(8,128)(2,1)}, bf16[512,512]{1,0:T(8,128)(2,1)}, f32[128,512]{1,0:T(8,128)}) custom-call(bf16[512,512]{1,0:T(8,128)(2,1)S(1)} %get-tuple-element.10.refs_0_, bf16[512,512]{1,0:T(8,128)(2,1)S(1)} %get-tuple-element.11.refs_1_, ...), custom_call_target="tpu_custom_call" | custom-call | tf_op jit(solution)/shard_map/write_out/pallas_call | solution.py:826

commit v4 on v3

--- a/solution.py
+++ b/solution.py
@@ -167,7 +167,7 @@
         weight_y(4)
 
     def head_columns(h):
-        return pl.ds(pl.multiple_of(h * DH, DH), DH)
+        return pl.ds(h * DH, DH)
 
     def scan_begin(n):
         loc[n] = tot[n].astype(BF16)
@@ -236,8 +236,7 @@
     loads[1].wait()
     loads[2].wait()
 
-    @pl.loop(0, HEADS)
-    def _(h):
+    for h in range(HEADS):
         cols = head_columns(h)
         tot[0, h] = dot(kb[:, cols], vb[:, cols], TN)
 
@@ -258,16 +257,14 @@
         jnp.int32, (ROWS, ROWS), 1
     )
 
-    @pl.loop(0, HEADS)
-    def _(h):
+    for h in range(HEADS):
         cols = head_columns(h)
         s = dot(scaled[:, cols], kb[:, cols], NT)
         scores[h] = jnp.where(causal, s, 0.0).astype(BF16)
 
     weight_1(4)
 
-    @pl.loop(0, HEADS)
-    def _(h):
+    for h in range(HEADS):
         cols = head_columns(h)
         gk_acc[:, cols] = dot(scores[h], vb[:, cols], NN)
 
@@ -283,8 +280,7 @@
     weight_3(4)
     scan_end(0, False)
 
-    @pl.loop(0, HEADS)
-    def _(h):
+    for h in range(HEADS):
         cols = head_columns(h)
         att[:, cols] = (dot(scaled[:, cols], state[0, h], NN) + gk_acc[:, cols]).astype(BF16)
 
@@ -623,8 +619,7 @@
     quarter_1(5)
     last_half(1)
 
-    @pl.loop(0, HEADS)
-    def _(h):
+    for h in range(HEADS):
         cols = head_columns(h)
         tot[1, h] = dot(scaled[:, cols], dab[:, cols], TN)
 
@@ -637,8 +632,7 @@
     quarter_3(1)
 
     def gradient_pair(start):
-        @pl.loop(start, start + 2)
-        def _(h):
+        for h in (start, start + 1):
             cols = head_columns(h)
             mixed = jnp.where(causal, dot(dab[:, cols], vb[:, cols], NT), 0.0).astype(BF16)
             g = dot(dab[:, cols], state[0, h], NT) + dot(mixed, kb[:, cols], NN)
@@ -663,8 +657,7 @@
     scan_end(1, True)
     out_copy.wait()
 
-    @pl.loop(0, HEADS)
-    def _(h):
+    for h in range(HEADS):
         cols = head_columns(h)
         ok[:, cols] = (gk_acc[:, cols] + dot(vb[:, cols], state[1, h], NT)).astype(BF16)
         ov[:, cols] = (gv_acc[:, cols] + dot(kb[:, cols], state[1, h], NN)).astype(BF16)

time: 127 us -> 125 us (0.984); the launches traced: 125 us -> 124 us
  no operation moved by 1% of the time
where the time goes in v4:
time: 125 us; the launch traced here: 124 us
  Pallas kernels  124 us (99%)
    pallas_call x1, Pallas kernels, on_device(): pl.pallas_call(body, out_shape=shapes, in_specs=[pl.BlockSpec(memory_spac...  122 us

profile of v4, /device:TPU:16, one launch (start us, length us, event | category | flops | bytes accessed | tf_op | source)
XLA Modules:
  0.0 124.5 jit_solution(3624306460700846391)
XLA Ops:
  0.6 122.2 %linear_attention.1 = (bf16[512,512]{1,0:T(8,128)(2,1)S(1)}, bf16[512,512]{1,0:T(8,128)(2,1)S(1)}, bf16[512,512]{1,0:T(8,128)(2,1)S(1)}, bf16[512,512]{1,0:T(8,128)(2,1)S(1)}, f32[128,512]{1,0:T(8,128)S(1)}) custom-call(bf16[512,512]{1,0:T(8,128)(2,1)} %refs_0_.1, bf16[512,512]{1,0:T(8,128)(2,1)} %refs_1_.1, bf16[512,512]{1,0:T(8,128)(2,1)} %refs_2_.1, ...), custom_call_target="tpu_custom_call" | custom-call | tf_op jit(solution)/shard_map/linear_attention/pallas_call | solution.py:808
  122.9 1.4 %write_out.1 = (bf16[512,512]{1,0:T(8,128)(2,1)}, bf16[512,512]{1,0:T(8,128)(2,1)}, bf16[512,512]{1,0:T(8,128)(2,1)}, bf16[512,512]{1,0:T(8,128)(2,1)}, f32[128,512]{1,0:T(8,128)}) custom-call(bf16[512,512]{1,0:T(8,128)(2,1)S(1)} %get-tuple-element.10.refs_0_, bf16[512,512]{1,0:T(8,128)(2,1)S(1)} %get-tuple-element.11.refs_1_, ...), custom_call_target="tpu_custom_call" | custom-call | tf_op jit(solution)/shard_map/write_out/pallas_call | solution.py:819

commit v5 on v4

--- a/solution.py
+++ b/solution.py
@@ -270,13 +270,14 @@
 
     scan_y(0, False)
 
-    @pl.when(jnp.logical_and(level_row(4) != y, level_row(3) != y))
+    weight_2(4)
+    weight_1(3)
+    scan_core(0, False)
+
+    @pl.when(level_row(2) == y)
     def _():
-        weight_y(1)
-
-    weight_1(3)
-    weight_2(4)
-    scan_core(0, False)
+        weight_y(2)
+
     weight_3(4)
     scan_end(0, False)
 
@@ -325,8 +326,13 @@
         reduce_copy(0, i).start()
         reduce_copy(1, i).start()
     weight_2(3)
+    weight_3(3)
     weight_1(2)
-    weight_3(3)
+
+    @pl.when(level_row(1) == y)
+    def _():
+        weight_y(1)
+
     weight_ready(3)
     partial(0, block(3))
     partial(1, block(-3))
@@ -335,10 +341,10 @@
         reduce_send(1, 2 + j, down_order[j], None if j < 2 else j - 2)
     for k in (2, 1):
         weight_2(k)
+        weight_3(k)
+        weight_ready(k)
         if k == 2:
             weight_1(1)
-        weight_3(k)
-        weight_ready(k)
         partial(0, block(k))
         partial(1, block(-k))
         for j in range(4):
@@ -593,7 +599,6 @@
     both_halves(1)
     piece_to_core(4).start()
     piece_to_core(5).start()
-    dw_3(2)
 
     b4 = block(4)
 
@@ -613,10 +618,9 @@
 
     last_half(0)
     last_weight_half(0)
-    quarter_2(2)
-    quarter_2(3)
     quarter_1(4)
     quarter_1(5)
+    dw_3(2)
     last_half(1)
 
     for h in range(HEADS):
@@ -625,6 +629,8 @@
 
     scan_begin(1)
     last_weight_half(1)
+    quarter_2(2)
+    quarter_2(3)
     scan_x(1)
     quarter_1(6)
     quarter_1(7)
@@ -651,9 +657,11 @@
     q_copy.start()
     quarter_2(6)
     quarter_2(7)
-    for p in range(4, 8):
-        quarter_3(p)
+    quarter_3(4)
+    quarter_3(5)
     scan_core(1, True)
+    quarter_3(6)
+    quarter_3(7)
     scan_end(1, True)
     out_copy.wait()
 

time: 125 us -> 125 us (level)
  no operation moved by 1% of the time
where the time goes in v5:
time: 125 us; the launch traced here: 124 us
  Pallas kernels  124 us (99%)
    pallas_call x1, Pallas kernels, on_device(): pl.pallas_call(body, out_shape=shapes, in_specs=[pl.BlockSpec(memory_spac...  122 us

profile of v5, /device:TPU:16, one launch (start us, length us, event | category | flops | bytes accessed | tf_op | source)
XLA Modules:
  0.0 124.4 jit_solution(18027978177548284161)
XLA Ops:
  0.6 122.2 %linear_attention.1 = (bf16[512,512]{1,0:T(8,128)(2,1)S(1)}, bf16[512,512]{1,0:T(8,128)(2,1)S(1)}, bf16[512,512]{1,0:T(8,128)(2,1)S(1)}, bf16[512,512]{1,0:T(8,128)(2,1)S(1)}, f32[128,512]{1,0:T(8,128)S(1)}) custom-call(bf16[512,512]{1,0:T(8,128)(2,1)} %refs_0_.1, bf16[512,512]{1,0:T(8,128)(2,1)} %refs_1_.1, bf16[512,512]{1,0:T(8,128)(2,1)} %refs_2_.1, ...), custom_call_target="tpu_custom_call" | custom-call | tf_op jit(solution)/shard_map/linear_attention/pallas_call | solution.py:816
  122.8 1.4 %write_out.1 = (bf16[512,512]{1,0:T(8,128)(2,1)}, bf16[512,512]{1,0:T(8,128)(2,1)}, bf16[512,512]{1,0:T(8,128)(2,1)}, bf16[512,512]{1,0:T(8,128)(2,1)}, f32[128,512]{1,0:T(8,128)}) custom-call(bf16[512,512]{1,0:T(8,128)(2,1)S(1)} %get-tuple-element.10.refs_0_, bf16[512,512]{1,0:T(8,128)(2,1)S(1)} %get-tuple-element.11.refs_1_, ...), custom_call_target="tpu_custom_call" | custom-call | tf_op jit(solution)/shard_map/write_out/pallas_call | solution.py:827

commit v6 on v5

--- a/solution.py
+++ b/solution.py
@@ -668,10 +668,14 @@
     for h in range(HEADS):
         cols = head_columns(h)
         ok[:, cols] = (gk_acc[:, cols] + dot(vb[:, cols], state[1, h], NT)).astype(BF16)
-        ov[:, cols] = (gv_acc[:, cols] + dot(kb[:, cols], state[1, h], NN)).astype(BF16)
 
     k_copy = pltpu.make_async_copy(ok, gk_o, out_sem.at[2])
     k_copy.start()
+
+    for h in range(HEADS):
+        cols = head_columns(h)
+        ov[:, cols] = (gv_acc[:, cols] + dot(kb[:, cols], state[1, h], NN)).astype(BF16)
+
     v_copy = pltpu.make_async_copy(ov, gv_o, out_sem.at[3])
     v_copy.start()
 

time: 125 us -> 125 us (level)
  no operation moved by 1% of the time
where the time goes in v6:
time: 125 us; the launch traced here: 124 us
  Pallas kernels  124 us (99%)
    pallas_call x1, Pallas kernels, on_device(): pl.pallas_call(body, out_shape=shapes, in_specs=[pl.BlockSpec(memory_spac...  122 us

profile of v6, /device:TPU:16, one launch (start us, length us, event | category | flops | bytes accessed | tf_op | source)
XLA Modules:
  0.0 124.4 jit_solution(10422889652854876485)
XLA Ops:
  0.6 122.2 %linear_attention.1 = (bf16[512,512]{1,0:T(8,128)(2,1)S(1)}, bf16[512,512]{1,0:T(8,128)(2,1)S(1)}, bf16[512,512]{1,0:T(8,128)(2,1)S(1)}, bf16[512,512]{1,0:T(8,128)(2,1)S(1)}, f32[128,512]{1,0:T(8,128)S(1)}) custom-call(bf16[512,512]{1,0:T(8,128)(2,1)} %refs_0_.1, bf16[512,512]{1,0:T(8,128)(2,1)} %refs_1_.1, bf16[512,512]{1,0:T(8,128)(2,1)} %refs_2_.1, ...), custom_call_target="tpu_custom_call" | custom-call | tf_op jit(solution)/shard_map/linear_attention/pallas_call | solution.py:820
  122.8 1.4 %write_out.1 = (bf16[512,512]{1,0:T(8,128)(2,1)}, bf16[512,512]{1,0:T(8,128)(2,1)}, bf16[512,512]{1,0:T(8,128)(2,1)}, bf16[512,512]{1,0:T(8,128)(2,1)}, f32[128,512]{1,0:T(8,128)}) custom-call(bf16[512,512]{1,0:T(8,128)(2,1)S(1)} %get-tuple-element.10.refs_0_, bf16[512,512]{1,0:T(8,128)(2,1)S(1)} %get-tuple-element.11.refs_1_, ...), custom_call_target="tpu_custom_call" | custom-call | tf_op jit(solution)/shard_map/write_out/pallas_call | solution.py:831
